TPU v7x, 256 devices: a whole 4x4x8 slice. The times are simulated.
256 devices in a mesh: sect: 64 (over z, y, core), tp: 4 (over x).
Axes of the slice: x: 4, y: 4, z: 8, core: 2. Of those that a mesh axis runs over, the one named last changes fastest.
Arguments:
- item_hidden: bfloat16 [4096, 4096], P('sect', 'tp'), may hold values from -40 to 40
- item_gain: bfloat16 [4096], P('tp'), may hold values from 0.25 to 1.75
- send_item: int32 [64, 64, 4], P('sect'), may hold values from -1 to 63, as said below
- pos_slot: int32 [256, 192], P('sect'), may hold values from 0 to 255, as said below
- hist_len: int32 [256], P('sect'), may hold values from 64 to 128, as said below
- user_gain: bfloat16 [4096], P('tp'), may hold values from 0.25 to 1.75
- query_weight: bfloat16 [4096, 4096], P('tp', 'sect'), may hold values from -0.09375 to 0.09375
Outputs:
- item_grad: float32 [4096, 4096], P('sect', 'tp')
- user_loss: float32 [256], P('sect')
Inputs may be any that keep to these rules, and one draw needn't show every extreme that they name: `send_item`: entry [o, r, s] names item o * 64 + value, owned by device o and sent to reader r, or is -1 for an empty slot. Within one (o, r) block the named items are distinct and the filled slots come first; at least half of the 4 slots (rounded down, and at least one) are filled. In every draw some reader gets 4 filled slots from every owner. `pos_slot`: entry [u, j] names a filled slot of the buffer of the device holding user u, in the order o * 4 + s; every filled slot is named by some candidate or some history position below that user's length. `hist_len`: every device's block of 4 users holds a user of length 128.
All inputs are finite; a program needn't handle non-finite values.
Results may differ from a plain program's by a relative error of at most 0.015.
Values may be sent and summed in bfloat16 or wider, within the bound.
A program may use at most 128 MiB of HBM per device.

v0:
```python
import jax
import jax.numpy as jnp
from jax import lax
from jax.sharding import PartitionSpec as P

D = 4096
HD = 128
CAND = 64


NORM_FLOOR = 1e-06
LOGIT_SOFTNESS = 20.0


def head_norm(values, head_count):
    shaped = values.reshape(values.shape[:-1] + (head_count, values.shape[-1] // head_count))
    return shaped * lax.rsqrt(jnp.mean(shaped * shaped, axis=-1, keepdims=True) + NORM_FLOOR)


def causal_mask(lengths, history_span):
    position = jnp.arange(history_span)
    allowed = (position[None, :] <= position[:, None])[None] & (
        position[None, None, :] < lengths[:, None, None]
    )
    return allowed.astype(jnp.float32)


def attend(query_rows, normed_rows, attend_mask):
    head_count = query_rows.shape[-1] // HD
    query_heads = head_norm(query_rows, head_count).astype(jnp.bfloat16)
    key_heads = head_norm(normed_rows, head_count).astype(jnp.bfloat16)
    value_heads = normed_rows.astype(jnp.bfloat16).reshape(query_heads.shape)
    scores = jnp.einsum(
        "uihd,ujhd->uhij", query_heads, key_heads, preferred_element_type=jnp.float32
    ) * HD ** (-0.5)
    weights = jnp.exp(scores) * attend_mask[:, None]
    weights = weights / jnp.sum(weights, axis=-1, keepdims=True)
    mixed_rows = jnp.einsum(
        "uhij,ujhd->uihd",
        weights.astype(jnp.bfloat16),
        value_heads,
        preferred_element_type=jnp.float32,
    )
    return mixed_rows.reshape(query_rows.shape)


def score_parts(mixed_rows, history_rows, cand_rows):
    outputs = history_rows + mixed_rows
    follow = jnp.concatenate([history_rows[:, 1:], jnp.zeros_like(history_rows[:, :1])], axis=1)
    own_squares = jnp.sum(outputs * outputs, axis=-1)
    positive_dot_products = jnp.sum(outputs * follow, axis=-1)
    negative_dot_products = jnp.einsum(
        "uif,ucf->uic", outputs, cand_rows, precision=lax.Precision.HIGHEST
    )
    return (own_squares, positive_dot_products, negative_dot_products)


def user_losses(
    own_squares,
    positive_dot_products,
    negative_dot_products,
    next_item_square_sums,
    candidate_square_sums,
    lengths,
):
    reciprocal_norm = lax.rsqrt(own_squares + NORM_FLOOR)
    positive_target_logit = (
        LOGIT_SOFTNESS
        * positive_dot_products
        * reciprocal_norm
        * lax.rsqrt(next_item_square_sums + NORM_FLOOR)
    )
    negative_score_logits = (
        LOGIT_SOFTNESS
        * negative_dot_products
        * reciprocal_norm[..., None]
        * lax.rsqrt(candidate_square_sums + NORM_FLOOR)[:, None, :]
    )
    partition = jnp.exp(positive_target_logit) + jnp.sum(jnp.exp(negative_score_logits), axis=-1)
    terms = jnp.log(partition) - positive_target_logit
    position = jnp.arange(own_squares.shape[1])
    allowed = position[None, :] < lengths[:, None] - 1
    return jnp.sum(jnp.where(allowed, terms, 0.0), axis=-1) / (lengths - 1).astype(jnp.float32)


def slot_norm(slot_rows, slot_squares, gain_row):
    return slot_rows * lax.rsqrt(slot_squares / D + NORM_FLOOR)[:, None] * gain_row


def segment_rows(values, places, count):
    return jax.ops.segment_sum(
        values.reshape((-1,) + values.shape[2:]), places.reshape(-1), num_segments=count
    )


def local(item_hidden, item_gain, send_item, pos_slot, hist_len, user_gain, query_weight):
    hidden = item_hidden.astype(jnp.float32)
    item_squares = lax.psum(jnp.sum(hidden * hidden, axis=1), "tp")
    embedded = (
        hidden * lax.rsqrt(item_squares / D + NORM_FLOOR)[:, None] * item_gain.astype(jnp.float32)
    ).astype(jnp.bfloat16)
    send_slots = send_item[0]
    vacant = send_slots < 0
    picked = jnp.take(embedded, jnp.where(vacant, 0, send_slots), axis=0)
    outgoing = jnp.where(vacant[..., None], jnp.zeros((), jnp.bfloat16), picked)
    arrived = lax.all_to_all(outgoing, "sect", split_axis=0, concat_axis=0, tiled=True)
    feature_count = arrived.shape[-1]
    slot_rows = arrived.reshape(-1, feature_count).astype(jnp.float32)
    slot_count = slot_rows.shape[0]
    slot_squares = lax.psum(jnp.sum(slot_rows * slot_rows, axis=1), "tp")
    gain_row = user_gain.astype(jnp.float32)

    def norm_only(rows_in, squares_in):
        return slot_norm(rows_in, squares_in, gain_row)

    normed_slots, norm_back = jax.vjp(norm_only, slot_rows, slot_squares)
    normed_low = normed_slots.astype(jnp.bfloat16)
    partial_query = jnp.dot(
        normed_low,
        lax.all_gather(query_weight, "sect", axis=1, tiled=True),
        preferred_element_type=jnp.float32,
    )
    query_slots = lax.psum_scatter(
        partial_query.astype(jnp.bfloat16), "tp", scatter_dimension=1, tiled=True
    ).astype(jnp.float32)
    history_span = pos_slot.shape[1] - CAND
    hist_places = pos_slot[:, :history_span]
    cand_places = pos_slot[:, history_span:]
    follow_places = jnp.concatenate([hist_places[:, 1:], hist_places[:, :1]], axis=1)
    history_rows = slot_rows[hist_places]
    cand_rows = slot_rows[cand_places]
    normed_rows = normed_low[hist_places].astype(jnp.float32)
    query_rows = query_slots[hist_places]
    attend_mask = causal_mask(hist_len, history_span)

    def attend_only(query_in, normed_in):
        return attend(query_in, normed_in, attend_mask)

    mixed_rows, attend_back = jax.vjp(attend_only, query_rows, normed_rows)
    partial_stats, parts_back = jax.vjp(score_parts, mixed_rows, history_rows, cand_rows)
    own_squares, positive_dot_products, negative_dot_products = (
        lax.psum(partial_stats[0].astype(jnp.bfloat16), "tp").astype(jnp.float32),
        lax.psum(partial_stats[1].astype(jnp.bfloat16), "tp").astype(jnp.float32),
        lax.psum(partial_stats[2].astype(jnp.bfloat16), "tp").astype(jnp.float32),
    )
    next_item_square_sums = slot_squares[follow_places]
    candidate_square_sums = slot_squares[cand_places]

    def loss_only(own_in, hit_in, neg_in, follow_in, cand_in):
        return user_losses(own_in, hit_in, neg_in, follow_in, cand_in, hist_len)

    losses, loss_back = jax.vjp(
        loss_only,
        own_squares,
        positive_dot_products,
        negative_dot_products,
        next_item_square_sums,
        candidate_square_sums,
    )
    grad_own, grad_hit, grad_neg, grad_follow, grad_cand = loss_back(
        jnp.full(losses.shape, float(D), jnp.float32)
    )
    grad_mixed, grad_history, grad_cands = parts_back((grad_own, grad_hit, grad_neg))
    grad_query, grad_normed = attend_back(grad_mixed)
    grad_slots = segment_rows(grad_history, hist_places, slot_count) + segment_rows(
        grad_cands, cand_places, slot_count
    )
    grad_squares = segment_rows(grad_follow, follow_places, slot_count) + segment_rows(
        grad_cand, cand_places, slot_count
    )
    grad_norm_slots = segment_rows(grad_normed, hist_places, slot_count)
    grad_query_slots = segment_rows(grad_query, hist_places, slot_count)
    every_query = lax.all_gather(grad_query_slots.astype(jnp.bfloat16), "tp", axis=1, tiled=True)
    grad_from_query = lax.dot_general(
        every_query,
        lax.all_gather(query_weight, "sect", axis=1, tiled=True),
        (((1,), (1,)), ((), ())),
        preferred_element_type=jnp.float32,
    )
    grad_norm_slots = grad_norm_slots + grad_from_query
    back_rows, back_squares = norm_back(grad_norm_slots)
    back_squares = lax.psum(back_squares, "tp")
    grad_slots = grad_slots + back_rows + 2.0 * slot_rows * (grad_squares + back_squares)[:, None]
    returned = lax.all_to_all(
        grad_slots.reshape(arrived.shape).astype(jnp.bfloat16),
        "sect",
        split_axis=0,
        concat_axis=0,
        tiled=True,
    ).astype(jnp.float32)
    item_count = embedded.shape[0]
    targets = jnp.where(vacant, item_count, send_slots).reshape(-1)
    item_grad = jax.ops.segment_sum(
        returned.reshape(-1, feature_count), targets, num_segments=item_count + 1
    )[:item_count]
    return (item_grad, losses)


def solution(mesh):
    placed = (
        P("sect", "tp"),
        P("tp"),
        P("sect", None, None),
        P("sect", None),
        P("sect"),
        P("tp"),
        P("tp", "sect"),
    )
    return jax.shard_map(
        local, mesh=mesh, in_specs=placed, out_specs=(P("sect", "tp"), P("sect")), check_vma=False
    )
```

profile of v0, /device:TPU:1, one launch (start us, length us, event | category | flops | bytes accessed | tf_op | source)
XLA Modules:
  0.0 333.5 jit_solution(12200618832667628850)
XLA Ops:
  11.4 9.3 %psum.42 = f32[64]{0:T(128)S(1)} all-reduce(f32[64]{0:T(128)S(1)} %fusion.29), channel_id=1, replica_groups=mesh['sect'=64,'tp'=4] {'tp'}, use_global_device_ids=true, to_apply=%region_1.0 | all-reduce | flops 64 | bytes 512 | tf_op jit(solution)/shard_map/psum | solution.py:98
  24.4 14.3 %all-to-all-start = ((bf16[64,4,1024]{2,1,0:T(4,128)(2,1)}), bf16[64,4,1024]{2,1,0:T(4,128)(2,1)S(1)}, u32[]{:S(2)}, u32[]{:S(2)}) async-start(bf16[64,4,1024]{2,1,0:T(4,128)(2,1)} %select_select_fusion), calls=%async_computation | async-start | bytes 1048576 | tf_op jit(solution)/shard_map/all_to_all | solution.py:106
  38.9 19.4 %all-to-all-done = bf16[64,4,1024]{2,1,0:T(4,128)(2,1)S(1)} async-done(((bf16[64,4,1024]{2,1,0:T(4,128)(2,1)}), bf16[64,4,1024]{2,1,0:T(4,128)(2,1)S(1)}, u32[]{:S(2)}, u32[]{:S(2)}) %all-to-all-start) | async-done | bytes 524320 | tf_op jit(solution)/shard_map/all_to_all | solution.py:106
  58.9 6.0 %psum.43 = f32[256]{0:T(256)S(1)} all-reduce(f32[256]{0:T(256)S(1)} %reduce_sum.141), channel_id=1, replica_groups=mesh['sect'=64,'tp'=4] {'tp'}, use_global_device_ids=true, to_apply=%region_3.4 | all-reduce | flops 256 | bytes 2048 | tf_op jit(solution)/shard_map/psum | solution.py:110
  65.1 34.8 %all-gather.3.cloned.1.call-done = bf16[1024,4096]{0,1:T(8,128)(2,1)} async-done(((bf16[1024,64]{0,1:T(8,128)(2,1)}), bf16[1024,4096]{0,1:T(8,128)(2,1)}) %all-gather.3.cloned.1.call-update) | async-done | bytes 8388624 | tf_op jit(solution)/shard_map/all_gather | solution.py:120
  99.9 7.2 %convolution_convert_fusion = bf16[256,4096]{1,0:T(8,128)(2,1)} fusion(bf16[256,1024]{1,0:T(8,128)(2,1)S(1)} %multiply_convert_fusion.1, bf16[1024,4096]{0,1:T(8,128)(2,1)} %all-gather.3.cloned.1.call-done), kind=kOutput, calls=%fused_computation.14 | convolution fusion | flops 2148532224 | bytes 11010048 | tf_op jit(solution)/shard_map/dot_general | solution.py:118
  113.9 2.8 gather_fusion.2
  121.6 2.7 gather_fusion.1
  124.3 3.4 %copy.133 = f32[64,8,8,128]{3,2,1,0:T(8,128)} copy(f32[64,8,8,128]{3,1,2,0:T(8,128)} %bitcast.107) | data formatting | bytes 4194304
  127.6 3.1 copy.113
  132.5 3.5 %gather_fusion.4 = f32[512]{0:T(512)S(1)} fusion(f32[256]{0:T(256)S(1)} %psum.43, s32[1024]{0:T(1024)S(1)} %pad_clamp_fusion.1), kind=kCustom, calls=%fused_computation.4 | custom fusion | bytes 6144 | tf_op jit(solution)/shard_map/gather | solution.py:146
  137.4 2.7 gather_fusion.3
  146.6 2.8 fusion.20
  152.8 3.2 multiply_reduce_fusion
  158.1 8.6 %all-reduce.2 = (bf16[4,128]{1,0:T(4,128)(2,1)S(1)}, bf16[4,128]{1,0:T(4,128)(2,1)S(1)}) all-reduce(bf16[4,128]{1,0:T(4,128)(2,1)S(1)} %get-tuple-element.27, bf16[4,128]{1,0:T(4,128)(2,1)S(1)} %get-tuple-element.10), channel_id=1, replica_groups=mesh['sect'=64,'tp'=4] {'tp'}, use_global_device_ids=true, to_apply=%region_11.12 | all-reduce | flops 1024 | bytes 4096 | tf_op jit(solution)/shard_map/psum | solution.py:142
  167.3 34.6 %all-reduce.5.cloned.1.call-done = bf16[4,128,64]{1,2,0:T(8,128)(2,1)} async-done(((bf16[4,128,64]{1,2,0:T(8,128)(2,1)}), bf16[4,128,64]{1,2,0:T(8,128)(2,1)}) %all-reduce.5.cloned.1.call-update) | async-done | bytes 65552 | tf_op jit(solution)/shard_map/psum | solution.py:144
  205.9 3.5 %pad_add_fusion = (f32[4,128,1024]{2,1,0:T(8,128)}, bf16[4,128,1024]{2,1,0:T(8,128)(2,1)}) fusion(f32[4,127,1024]{2,1,0:T(8,128)S(1)} %slice_multiply_fusion, f32[4,128,1024]{2,1,0:T(8,128)S(1)} %get-tuple-element.11, f32[4,128]{1,0:T(4,128)S(1)} %multiply_multiply_fusion.5, f32[4,127,1024]{2,1,0:T(8,128)S(1)} %copy-done.3, ...), kind=kOutput, calls=%fused_computation.48 | convolution fusion | flops 406552576 | bytes 10005504 | tf_op jit(solution)/shard_map/transpose(jvp(uif,ucf->uic))/dot_general | solution.py:52
  211.6 3.2 fusion.5
  218.5 2.9 copy.120
  221.4 7.5 %scatter_custom_fusion.2 = f32[256,1024]{1,0:T(8,128)} fusion(s32[512]{0:T(512)} %get-tuple-element.20, f32[64,8,8,128]{3,2,1,0:T(8,128)} %bitcast.114, f32[]{:T(128)} %constant.17.clone.1), kind=kCustom, calls=%fused_computation.37 | custom fusion | flops 524288 | bytes 3146240 | tf_op jit(solution)/shard_map/scatter-add | solution.py:91
  231.2 4.3 %fusion.9 = (f32[4,128,8]{1,2,0:T(8,128)S(1)}, bf16[4,8,128,128]{2,3,1,0:T(8,128)(2,1)S(1)}) fusion(bf16[4,128,8,128]{1,3,2,0:T(8,128)(2,1)} %copy.110, f32[4,128,8,128]{1,3,2,0:T(8,128)} %copy-done.1, f32[4,128,8]{1,2,0:T(8,128)S(1)} %get-tuple-element.37, bf16[4,8,128,128]{2,3,1,0:T(8,128)(2,1)} %copy-done.17, f32[4,8,128,128]{2,3,1,0:T(8,128)} %copy-done.9, ...), kind=kOutput, calls=%fused_computation.33 | convolution fusion | flops 141553664 | bytes 7667712 | tf_op jit(solution)/shard_map/transpose(jvp(uihd,ujhd->uhij))/dot_general | solution.py:33
  237.9 3.0 copy.123
  245.6 4.4 %scatter_custom_fusion.1 = f32[256,1024]{1,0:T(8,128)} fusion(s32[256]{0:T(256)S(1)} %reshape.374, f32[256,1024]{1,0:T(8,128)} %bitcast.124, f32[]{:T(128)} %constant.17.clone.1), kind=kCustom, calls=%fused_computation.68 | custom fusion | flops 262144 | bytes 1049088 | tf_op jit(solution)/shard_map/scatter-add | solution.py:91
  250.0 6.8 %scatter_custom_fusion = f32[256,1024]{1,0:T(8,128)} fusion(s32[512]{0:T(512)} %get-tuple-element.20, f32[512,1024]{1,0:T(8,128)} %bitcast.123, f32[]{:T(128)} %constant.17.clone.1), kind=kCustom, calls=%fused_computation.70 | custom fusion | flops 524288 | bytes 1049088 | tf_op jit(solution)/shard_map/scatter-add | solution.py:91
  256.8 4.2 %scatter_custom_fusion.4 = f32[256]{0:T(256)S(1)} fusion(s32[512]{0:T(512)S(1)} %add_bitcast_fusion, f32[512]{0:T(512)} %get-tuple-element.6, f32[]{:T(128)} %constant.17.clone.1), kind=kCustom, calls=%fused_computation.158 | custom fusion | flops 512 | bytes 1536 | tf_op jit(solution)/shard_map/scatter-add | solution.py:91
  261.1 5.7 %all-gather.5.cloned.1.call-done = bf16[256,4096]{1,0:T(8,128)(2,1)} async-done(((bf16[256,1024]{1,0:T(8,128)(2,1)}), bf16[256,4096]{1,0:T(8,128)(2,1)}) %all-gather.5.cloned.1.call-update) | async-done | bytes 2097168 | tf_op jit(solution)/shard_map/all_gather | solution.py:173
  266.8 7.4 %fusion.78 = f32[256,1024]{1,0:T(8,128)} fusion(bf16[256,4096]{1,0:T(8,128)(2,1)} %all-gather.5.cloned.1.call-done, bf16[1024,4096]{0,1:T(8,128)(2,1)} %all-gather.3.cloned.1.call-done), kind=kOutput, calls=%fused_computation.172 | convolution fusion | flops 2147483648 | bytes 11534336 | tf_op jit(solution)/shard_map/dot_general | solution.py:174
  274.2 7.4 %scatter_custom_fusion.3 = f32[256,1024]{1,0:T(8,128)} fusion(f32[256,1024]{1,0:T(8,128)} %fusion.78, s32[512]{0:T(512)} %get-tuple-element.20, f32[64,8,8,128]{3,2,1,0:T(8,128)S(1)} %bitcast.113), kind=kCustom, calls=%fused_computation.34 | custom fusion | flops 524288 | bytes 3145728 | tf_op jit(solution)/shard_map/scatter-add | solution.py:91
  283.1 6.6 %psum.47 = f32[256]{0:T(256)S(1)} all-reduce(f32[256]{0:T(256)S(1)} %multiply_multiply_fusion.7), channel_id=1, replica_groups=mesh['sect'=64,'tp'=4] {'tp'}, use_global_device_ids=true, to_apply=%region_26.27 | all-reduce | flops 256 | bytes 2048 | tf_op jit(solution)/shard_map/psum | solution.py:182
  292.7 12.9 %all-to-all-start.1 = ((bf16[64,4,1024]{2,1,0:T(4,128)(2,1)}), bf16[64,4,1024]{2,1,0:T(4,128)(2,1)S(1)}, u32[]{:S(2)}, u32[]{:S(2)}) async-start(bf16[64,4,1024]{2,1,0:T(4,128)(2,1)} %convert_element_type.151), calls=%async_computation.2 | async-start | bytes 1048576 | tf_op jit(solution)/shard_map/all_to_all | solution.py:184
  306.3 16.9 %all-to-all-done.1 = bf16[64,4,1024]{2,1,0:T(4,128)(2,1)S(1)} async-done(((bf16[64,4,1024]{2,1,0:T(4,128)(2,1)}), bf16[64,4,1024]{2,1,0:T(4,128)(2,1)S(1)}, u32[]{:S(2)}, u32[]{:S(2)}) %all-to-all-start.1) | async-done | bytes 524320 | tf_op jit(solution)/shard_map/all_to_all | solution.py:184
  323.3 2.7 scatter_custom_fusion.6
  (180 shorter events, 61.1 us)
Async XLA Ops:
  7.2 92.7 %all-gather.3.cloned.1.call-start = ((), (), s32[]{:S(2)}) async-start(), calls=%async_computation.3 | async-start | bytes 8519680 | tf_op jit(solution)/shard_map/all_gather | solution.py:120
  22.9 15.9 %copy-start.39 = (bf16[1024]{0:T(1024)(128)(2,1)S(1)}, bf16[1024]{0:T(1024)(128)(2,1)}, u32[]{:S(2)}) copy-start(bf16[1024]{0:T(1024)(128)(2,1)} %param.12) | copy-start | bytes 6148
  24.4 33.8 %all-to-all-start = ((bf16[64,4,1024]{2,1,0:T(4,128)(2,1)}), bf16[64,4,1024]{2,1,0:T(4,128)(2,1)S(1)}, u32[]{:S(2)}, u32[]{:S(2)}) async-start(bf16[64,4,1024]{2,1,0:T(4,128)(2,1)} %select_select_fusion), calls=%async_computation | async-start | bytes 1048576 | tf_op jit(solution)/shard_map/all_to_all | solution.py:106
  38.8 97.4 %reduce-scatter.2.cloned.1.call-start = ((), (), s32[]{:S(2)}) async-start(), calls=%async_computation.4 | async-start | bytes 2621440 | tf_op jit(solution)/shard_map/reduce_scatter | solution.py:123
  64.9 35.0 %copy-start.31 = (f32[256]{0:T(256)}, f32[256]{0:T(256)S(1)}, u32[]{:S(2)}) copy-start(f32[256]{0:T(256)S(1)} %fusion.65) | copy-start | bytes 3076
  107.1 94.7 %all-reduce.5.cloned.1.call-start = ((), (), s32[]{:S(2)}) async-start(), calls=%async_computation.5 | async-start | bytes 131072 | tf_op jit(solution)/shard_map/psum | solution.py:144
  113.9 18.5 %copy-start.29 = (f32[256]{0:T(256)}, f32[256]{0:T(256)S(1)}, u32[]{:S(2)}) copy-start(f32[256]{0:T(256)S(1)} %gather_fusion.6) | copy-start | bytes 3076
  132.4 3.6 %copy-start.5 = (bf16[4,128,8,128]{1,3,2,0:T(8,128)(2,1)S(1)}, bf16[4,128,8,128]{1,3,2,0:T(8,128)(2,1)}, u32[]{:S(2)}) copy-start(bf16[4,128,8,128]{1,3,2,0:T(8,128)(2,1)} %copy.110) | copy-start | bytes 3145732
  146.5 3.5 %copy-start.6 = (bf16[4,128,8,128]{1,3,2,0:T(8,128)(2,1)S(1)}, bf16[4,128,8,128]{1,3,2,0:T(8,128)(2,1)}, u32[]{:S(2)}) copy-start(bf16[4,128,8,128]{1,3,2,0:T(8,128)(2,1)} %copy.110) | copy-start | bytes 3145732
  146.5 3.5 %copy-start.15 = (f32[4,128,8,128]{1,3,2,0:T(8,128)S(1)}, f32[4,128,8,128]{1,3,2,0:T(8,128)}, u32[]{:S(2)}) copy-start(f32[4,128,8,128]{1,3,2,0:T(8,128)} %copy.113) | copy-start | bytes 6291460
  158.0 108.7 %all-gather.5.cloned.1.call-start = ((), (), s32[]{:S(2)}) async-start(), calls=%async_computation.6 | async-start | bytes 2621440 | tf_op jit(solution)/shard_map/all_gather | solution.py:173
  166.7 37.5 %copy-start.27 = (bf16[4,128]{1,0:T(4,128)(2,1)}, bf16[4,128]{1,0:T(4,128)(2,1)S(1)}, u32[]{:S(2)}) copy-start(bf16[4,128]{1,0:T(4,128)(2,1)S(1)} %get-tuple-element.4) | copy-start | bytes 3076
  166.7 37.5 %copy-start.33 = (bf16[4,128]{1,0:T(4,128)(2,1)}, bf16[4,128]{1,0:T(4,128)(2,1)S(1)}, u32[]{:S(2)}) copy-start(bf16[4,128]{1,0:T(4,128)(2,1)S(1)} %get-tuple-element.5) | copy-start | bytes 3076
  211.6 3.3 copy-start.2
  211.6 3.3 copy-start.7
  211.6 3.8 %copy-start.10 = (f32[4,8,128,128]{2,3,1,0:T(8,128)S(1)}, f32[4,8,128,128]{2,3,1,0:T(8,128)}, u32[]{:S(2)}) copy-start(f32[4,8,128,128]{2,3,1,0:T(8,128)} %copy-done.9) | copy-start | bytes 6291460
  211.6 3.8 %copy-start.20 = (f32[4,128,8]{1,2,0:T(8,128)S(1)}, f32[4,128,8]{1,2,0:T(8,128)}, u32[]{:S(2)}) copy-start(f32[4,128,8]{1,2,0:T(8,128)} %copy-done.19) | copy-start | bytes 49156
  221.4 9.6 %copy-start.37 = (s32[4,64]{1,0:T(4,128)S(1)}, s32[4,64]{1,0:T(4,128)}, u32[]{:S(2)}) copy-start(s32[4,64]{1,0:T(4,128)} %get-tuple-element.17) | copy-start | bytes 3076
  221.4 9.7 %copy-start.35 = (s32[4,127]{1,0:T(4,128)S(1)}, s32[4,127]{1,0:T(4,128)}, u32[]{:S(2)}) copy-start(s32[4,127]{1,0:T(4,128)} %get-tuple-element.13) | copy-start | bytes 6100
  221.4 9.7 %copy-start.36 = (s32[4,1]{1,0:T(4,128)S(1)}, s32[4,1]{1,0:T(4,128)}, u32[]{:S(2)}) copy-start(s32[4,1]{1,0:T(4,128)} %get-tuple-element.15) | copy-start | bytes 52
  231.2 4.3 %copy-start.8 = (bf16[4,128,8,128]{1,3,2,0:T(8,128)(2,1)S(1)}, bf16[4,128,8,128]{1,3,2,0:T(8,128)(2,1)}, u32[]{:S(2)}) copy-start(bf16[4,128,8,128]{1,3,2,0:T(8,128)(2,1)} %copy.110) | copy-start | bytes 3145732
  231.2 4.3 %copy-start.11 = (f32[4,8,128,128]{2,3,1,0:T(8,128)S(1)}, f32[4,8,128,128]{2,3,1,0:T(8,128)}, u32[]{:S(2)}) copy-start(f32[4,8,128,128]{2,3,1,0:T(8,128)} %copy-done.9) | copy-start | bytes 6291460
  231.2 4.3 %copy-start.14 = (bf16[4,128,1024]{1,2,0:T(8,128)(2,1)S(1)}, bf16[4,128,1024]{1,2,0:T(8,128)(2,1)}, u32[]{:S(2)}) copy-start(bf16[4,128,1024]{1,2,0:T(8,128)(2,1)} %copy.130) | copy-start | bytes 3145732
  237.9 5.4 %copy-start.22 = (f32[4,128]{1,0:T(4,128)S(1)}, f32[4,128]{1,0:T(4,128)}, u32[]{:S(2)}) copy-start(f32[4,128]{1,0:T(4,128)} %copy-done.21) | copy-start | bytes 6148
  237.9 5.4 %copy-start.25 = (f32[4,128]{1,0:T(4,128)S(1)}, f32[4,128]{1,0:T(4,128)}, u32[]{:S(2)}) copy-start(f32[4,128]{1,0:T(4,128)} %get-tuple-element.23) | copy-start | bytes 6148
  261.0 13.1 %copy-start.12 = (f32[4,128,8,128]{3,2,1,0:T(8,128)S(1)}, f32[4,128,8,128]{3,2,1,0:T(8,128)}, u32[]{:S(2)}) copy-start(f32[4,128,8,128]{3,2,1,0:T(8,128)} %copy.123) | copy-start | bytes 6291460
  274.2 15.6 %copy-start.32 = (f32[256]{0:T(256)S(1)}, f32[256]{0:T(256)}, u32[]{:S(2)}) copy-start(f32[256]{0:T(256)} %copy-done.31) | copy-start | bytes 3076
  281.6 8.2 %copy-start.13 = (f32[256,1024]{1,0:T(8,128)S(1)}, f32[256,1024]{1,0:T(8,128)}, u32[]{:S(2)}) copy-start(f32[256,1024]{1,0:T(8,128)} %scatter_custom_fusion.1) | copy-start | bytes 3145732
  291.7 13.9 %copy-start.23 = (s32[1,64,4]{1,2,0:T(4,128)S(1)}, s32[1,64,4]{1,2,0:T(4,128)}, u32[]{:S(2)}) copy-start(s32[1,64,4]{1,2,0:T(4,128)} %param.9) | copy-start | bytes 3076
  291.7 14.1 %copy-start.40 = (f32[4]{0:T(128)S(1)}, f32[4]{0:T(128)}, u32[]{:S(2)}) copy-start(f32[4]{0:T(128)} %get-tuple-element.12) | copy-start | bytes 52
  291.7 14.1 %copy-start.42 = (s32[4]{0:T(128)S(1)}, s32[4]{0:T(128)}, u32[]{:S(2)}) copy-start(s32[4]{0:T(128)} %param.11) | copy-start | bytes 52
  292.7 30.5 %all-to-all-start.1 = ((bf16[64,4,1024]{2,1,0:T(4,128)(2,1)}), bf16[64,4,1024]{2,1,0:T(4,128)(2,1)S(1)}, u32[]{:S(2)}, u32[]{:S(2)}) async-start(bf16[64,4,1024]{2,1,0:T(4,128)(2,1)} %convert_element_type.151), calls=%async_computation.2 | async-start | bytes 1048576 | tf_op jit(solution)/shard_map/all_to_all | solution.py:184
  (17 other events, 35.8 us)
Sparse Core Ops, SparseCore 0:
  10.7 89.1 all-gather.2
  107.3 28.5 reduce-scatter.1
  158.1 43.6 all-reduce.4
  231.1 35.5 all-gather.4
where the time goes:
time: 339 us; the launch traced here: 333 us
  waiting for transfers between devices  112 us (33%)
  other arithmetic  61.6 us (18%)
  local copies, waits for them, and re-layouts  50 us (15%)
  matrix products  37 us (11%)
  blocking collectives  30.5 us (9%)
  starting transfers between devices  27.5 us (8%)
  between operations  14.6 us (4%)
    all_gather x1, waiting for transfers between devices, local(): lax.all_gather(query_weight, 'sect', axis=1, tiled=True)  34.8 us
    psum x1, waiting for transfers between devices, local(): lax.psum(partial_stats[2].astype(jnp.bfloat16), 'tp').astype(jnp.float32)  34.6 us
    scatter-add x6, other arithmetic, segment_rows(): jax.ops.segment_sum(values.reshape((-1,) + values.shape[2:]), places.resh...  32.6 us
    all_to_all x1, waiting for transfers between devices, local(): lax.all_to_all(outgoing, 'sect', split_axis=0, concat_axis=0, tiled=True)  19.4 us
    all_to_all x1, waiting for transfers between devices, local(): lax.all_to_all(grad_slots.reshape(arrived.shape).astype(jnp.bfloat16), 's...  16.9 us
    all_to_all x1, starting transfers between devices, local(): lax.all_to_all(outgoing, 'sect', split_axis=0, concat_axis=0, tiled=True)  14.3 us
    all_to_all x1, starting transfers between devices, local(): lax.all_to_all(grad_slots.reshape(arrived.shape).astype(jnp.bfloat16), 's...  12.9 us
    unnamed x90, local copies, waits for them, and re-layouts  9.68 us
  transfers between devices with their start and end apart: 6, of which 5 were waited for; matrix products, arithmetic and copies ran while one was open for 20% of the time, Pallas kernels for 0%

commit v1 on v0

v1 whole, which is shorter than its diff:
```python
import jax
import jax.numpy as jnp
from jax import lax
from jax.experimental import pallas as pl
from jax.experimental.pallas import tpu as pltpu
from jax.sharding import PartitionSpec as P

D = 4096
HD = 128
HIST = 128
CAND = 64
NZ, NY, NT = 8, 4, 4
NS = 64
EPS = 1e-06
SOFT = 20.0
F32, BF16 = jnp.float32, jnp.bfloat16
HI = lax.Precision.HIGHEST
MESH = pl.DeviceIdType.MESH
RING = (4, 3, 3, 4)


def mm(a, b, ca, cb, precision=None):
    return lax.dot_general(
        a, b, (((ca,), (cb,)), ((), ())), preferred_element_type=F32, precision=precision
    )


def columns(row):
    return mm(row, jnp.full((8, 128), 0.125, F32), 0, 0, HI)


def lane_sum(values):
    return jnp.sum(values, axis=1, keepdims=True)


def iota(shape, dim):
    return lax.broadcasted_iota(jnp.int32, shape, dim)


def one_hot(row, count):
    return jnp.where(iota((count, row.shape[1]), 0) == row, 1.0, 0.0)


def norm_heads(values):
    heads, roots = [], []
    for par in range(2):
        part = values[:, par * HD : (par + 1) * HD]
        root = lax.rsqrt(lane_sum(part * part) * (1.0 / HD) + EPS)
        heads.append(part * root)
        roots.append(root)
    return heads, roots


def norm_heads_back(values, grads):
    heads, roots = norm_heads(values)
    out = []
    for par in range(2):
        grad = grads[:, par * HD : (par + 1) * HD]
        out.append(
            roots[par] * (grad - heads[par] * (lane_sum(grad * heads[par]) * (1.0 / HD)))
        )
    return jnp.concatenate(out, axis=1)


def kernel(
    len_ref, hidden_ref, w_ref, gi_ref, gu_ref, sel_ref, pos_ref,
    grad_ref, loss_ref,
    hd, selb, wt, sqx, ps, pr, oute, outq, bufe, bufq, gt, nrm, knb, ssx, sqm, q32,
    rcol, rscol,
    rows_s, cand_s, kn_s, v_s, qn_s, w_s, o_s, st_r,
    aq, ak, av, ae, gsq, dqo, eo, rq, re, dqg, gws, gwr, es, er, nbx, nwx,
    xs, xr, ys, yr, ring_s, ring_r, par_s, par_r, a2a_s, a2a_r,
):
    me = lax.axis_index("sect")
    t = lax.axis_index("tp")
    z, y, c = me // 8, (me // 2) % 4, me % 2
    blk = z * 2 + c

    def send(src, dst, ssem, rsem, sect, tp):
        return pltpu.make_async_remote_copy(
            src_ref=src, dst_ref=dst, send_sem=ssem, recv_sem=rsem,
            device_id=(sect, tp), device_id_type=MESH,
        )

    def sect_of(zz, yy, cc):
        return zz * 8 + yy * 2 + cc

    def x_copy(k, src, dst, j):
        peer = (t + j) % NT
        return send(src(peer), dst.at[t], xs.at[k, j], xr.at[k, j], me, peer)

    def x_from(k, src, dst, j):
        sender = (t + NT - j) % NT
        return send(src(t), dst.at[sender], xs.at[k, j], xr.at[k, j], me, sender)

    def y_copy(k, src, dst, j):
        peer = (y + j) % NY
        return send(src(peer), dst.at[y], ys.at[k, j], yr.at[k, j], sect_of(z, peer, c), t)

    def y_from(k, src, dst, j):
        sender = (y + NY - j) % NY
        return send(src(y), dst.at[sender], ys.at[k, j], yr.at[k, j], sect_of(z, sender, c), t)

    def start3(copy, k, src, dst):
        for j in (2, 1, 3):
            copy(k, src, dst, j).start()

    def wait_in(came, k, src, dst):
        for j in (1, 3, 2):
            came(k, src, dst, j).wait_recv()

    def wait_out(copy, k, src, dst):
        for j in (1, 3, 2):
            copy(k, src, dst, j).wait_send()

    def rows_of(first):
        return pl.ds(pl.multiple_of(first * 16, 16), 16)

    def to_readers(k, out, buf):
        pltpu.make_async_copy(
            out.at[rows_of(me)], buf.at[y, rows_of(blk)], a2a_r.at[k]
        ).start()

        def step(j, carry):
            peer = (me + j) % NS
            send(
                out.at[rows_of(peer)], buf.at[y, rows_of(blk)], a2a_s.at[k], a2a_r.at[k], peer, t
            ).start()
            return carry

        lax.fori_loop(1, NS, step, 0)

    def to_groups(k, out, buf):
        pltpu.make_async_copy(
            out.at[y, rows_of(blk)], buf.at[rows_of(me)], a2a_r.at[k]
        ).start()

        def step(j, carry):
            peer = (me + j) % NS
            pz, py, pc = peer // 8, (peer // 2) % 4, peer % 2
            send(
                out.at[py, rows_of(pz * 2 + pc)], buf.at[rows_of(me)],
                a2a_s.at[k], a2a_r.at[k], peer, t,
            ).start()
            return carry

        lax.fori_loop(1, NS, step, 0)

    def all_in(k, buf):
        pltpu.make_async_copy(buf, buf, a2a_r.at[k]).wait()

    def all_out(k, flat):
        part = flat.at[pl.ds(0, (NS - 1) * 16)]
        pltpu.make_async_copy(part, part, a2a_s.at[k]).wait()

    def ring(stream, step):
        way = 1 if stream < 2 else NZ - 1
        block = (z + (NZ - way) * step) % NZ
        part = wt.at[block, c, pl.ds((stream % 2) * 32, 32)]
        return send(
            part, part, ring_s.at[stream, step], ring_r.at[stream, step],
            sect_of((z + way) % NZ, y, c), t,
        )

    def ring_from(stream, step):
        way = 1 if stream < 2 else NZ - 1
        block = (z + (NZ - way) * (step + 1)) % NZ
        part = wt.at[block, c, pl.ds((stream % 2) * 32, 32)]
        return block, send(
            part, part, ring_s.at[stream, step], ring_r.at[stream, step],
            sect_of((z + way) % NZ, y, c), t,
        )

    def partner(block, core, half):
        part = wt.at[block, core, pl.ds(half * 32, 32)]
        return send(
            part, part, par_s.at[block, half], par_r.at[block, half], sect_of(z, y, 1 - c), t
        )

    def advance(step):
        for stream in range(4):
            if step >= RING[stream]:
                continue
            block, came = ring_from(stream, step)
            came.wait_recv()
            if step + 1 < RING[stream]:
                ring(stream, step + 1).start()
            partner(block, c, stream % 2).start()

    barrier = pltpu.get_barrier_semaphore()

    def greet(j, carry):
        pl.semaphore_signal(barrier, inc=1, device_id=((me + j) % NS, t), device_id_type=MESH)
        return carry

    lax.fori_loop(1, NS, greet, 0)
    for j in range(1, NT):
        pl.semaphore_signal(barrier, inc=1, device_id=(me, (t + j) % NT), device_id_type=MESH)

    hd[y] = hidden_ref[...]
    selb[y] = sel_ref[...]
    eye = jnp.where(iota((64, 64), 0) == iota((64, 64), 1), 1.0, 0.0).astype(BF16)
    wt[z, c] = mm(eye, w_ref[...], 1, 1).astype(BF16)
    for ref in (aq, ak, av, ae):
        ref[...] = jnp.zeros(ref.shape, F32)
    gsq[...] = jnp.zeros(gsq.shape, F32)
    pl.semaphore_wait(barrier, NS - 1 + NT - 1)

    own_hd = lambda peer: hd.at[y]
    own_sel = lambda peer: selb.at[y]
    for stream in range(4):
        ring(stream, 0).start()
    start3(y_copy, 0, own_hd, hd)
    start3(y_copy, 1, own_sel, selb)
    for half in range(2):
        partner(z, c, half).start()
    advance(0)
    advance(1)

    wait_in(y_from, 0, own_hd, hd)
    gi = gi_ref[...].astype(F32)
    gu = gu_ref[...].astype(F32)
    ones = jnp.ones((8, 1024), F32)
    hidden = hd[...].reshape(256, 1024).astype(F32)
    gained = hidden * gi
    sqx[t, pl.ds(0, 8), :] = mm(ones, hidden * hidden, 1, 1, HI)
    sqx[t, pl.ds(8, 8), :] = mm(ones, gained * gained, 1, 1, HI)
    own_sqx = lambda peer: sqx.at[t]
    start3(x_copy, 0, own_sqx, sqx)
    wait_in(y_from, 1, own_sel, selb)
    picks = jnp.maximum(jnp.maximum(selb[0], selb[1]), jnp.maximum(selb[2], selb[3]))
    gt[...] = one_hot(picks, 256).astype(BF16)
    advance(2)
    wait_in(x_from, 0, own_sqx, sqx)
    sums = sqx[0] + sqx[1] + sqx[2] + sqx[3]
    r_row = lax.rsqrt(sums[0:8] * (1.0 / D) + EPS)
    rs_row = lax.rsqrt(r_row * r_row * sums[8:16] * (1.0 / D) + EPS)
    rcol[...] = columns(r_row)
    rscol[...] = columns(rs_row)
    pieces = []
    for par in range(2):
        lanes = pl.ds(pl.multiple_of((par * 4 + y) * HD, HD), HD)
        piece = hd[:, :, lanes].reshape(256, HD).astype(F32)
        gain = gi_ref[:, lanes].astype(F32)
        pieces.append((piece * rcol[...] * gain).astype(BF16))
    oute[...] = mm(gt[...], jnp.concatenate(pieces, axis=1), 0, 0).astype(BF16)
    to_readers(0, oute, bufe)

    lhs = (hd[...].reshape(256, 1024).astype(F32) * (gi * gu)).astype(BF16)
    advance(3)
    for b in range(NZ):
        for half in range(2):
            partner(b, 1 - c, half).wait_recv()
    ps_of = lambda peer: ps.at[peer]
    for tt in range(NT):
        block = wt[2 * tt : 2 * tt + 2].reshape(256, 1024)
        ps[tt] = mm(lhs, block, 1, 1).astype(BF16)
    start3(x_copy, 1, ps_of, pr)
    pr[t] = ps[t]
    wait_in(x_from, 1, ps_of, pr)
    total = (
        pr[0].astype(F32) + pr[1].astype(F32) + pr[2].astype(F32) + pr[3].astype(F32)
    ) * (rcol[...] * rscol[...])[:, 0:1]
    q32[...] = total
    heads, _ = norm_heads(total)
    outq[...] = mm(gt[...], jnp.concatenate(heads, axis=1).astype(BF16), 0, 0).astype(BF16)
    to_readers(1, outq, bufq)

    all_in(0, bufe)
    ones_q = jnp.ones((8, 256), F32)
    part = jnp.zeros((8, 256), F32)
    for q in range(4):
        rows = bufe[q].astype(F32)
        part = part + mm(ones_q, rows * rows, 1, 1, HI)
    ssx[t] = part
    own_ssx = lambda peer: ssx.at[t]
    start3(x_copy, 2, own_ssx, ssx)

    def gain_of(q):
        return jnp.concatenate(
            [gu[:, q * HD : (q + 1) * HD], gu[:, (4 + q) * HD : (5 + q) * HD]], axis=1
        )

    def hist_hot(u):
        return one_hot(pos_ref[u], 256)

    def cand_hot(u):
        return one_hot(pos_ref[4 + u], 256)

    wait_in(x_from, 2, own_ssx, ssx)
    sq_row = ssx[0] + ssx[1] + ssx[2] + ssx[3]
    sqm[...] = columns(sq_row)
    rs = lax.rsqrt(sqm[...] * (1.0 / D) + EPS)[:, 0:1]
    for q in range(4):
        low = (bufe[q].astype(F32) * rs * gain_of(q)).astype(BF16)
        nrm[q] = low
        heads, _ = norm_heads(low.astype(F32))
        knb[q] = jnp.concatenate(heads, axis=1).astype(BF16)

    def gather_user(u, carry):
        hot = hist_hot(u).astype(BF16)
        hot_c = cand_hot(u).astype(BF16)
        for q in range(4):
            rows_s[u, q] = mm(hot, bufe[q], 0, 0).astype(BF16)
            cand_s[u, q] = mm(hot_c, bufe[q], 0, 0).astype(BF16)
            kn_s[u, q] = mm(hot, knb[q], 0, 0).astype(BF16)
            v_s[u, q] = mm(hot, nrm[q], 0, 0).astype(BF16)
        return carry

    lax.fori_loop(0, 4, gather_user, 0)
    all_in(1, bufq)

    scale = HD ** (-0.5)
    row_id = iota((HIST, HIST), 0)
    col_id = iota((HIST, HIST), 1)

    def follow_of(rows):
        moved = pltpu.roll(rows, HIST - 1, 0)
        return jnp.where(iota(rows.shape, 0) < HIST - 1, moved, 0.0)

    def st_copy(u, j):
        peer = (t + j) % NT
        return send(st_r.at[t, u], st_r.at[t, u], xs.at[8 + u, j], xr.at[8 + u, j], me, peer)

    def st_from(u, j):
        sender = (t + NT - j) % NT
        return send(
            st_r.at[t, u], st_r.at[sender, u], xs.at[8 + u, j], xr.at[8 + u, j], me, sender
        )

    def forward_user(u, carry):
        hot = hist_hot(u).astype(BF16)
        mask = jnp.where((col_id <= row_id) & (col_id < len_ref[u]), 1.0, 0.0)
        own = jnp.zeros((HIST, 1), F32)
        hit = jnp.zeros((HIST, 1), F32)
        neg = jnp.zeros((HIST, HIST), F32)
        for q in range(4):
            qn = mm(hot, bufq[q], 0, 0).astype(BF16)
            qn_s[u, q] = qn
            kn = kn_s[u, q]
            val = v_s[u, q]
            mixed = []
            for par in range(2):
                lanes = slice(par * HD, (par + 1) * HD)
                weights = jnp.exp(mm(qn[:, lanes], kn[:, lanes], 1, 1) * scale) * mask
                weights = (weights / lane_sum(weights)).astype(BF16)
                w_s[u, 2 * q + par] = weights
                mixed.append(mm(weights, val[:, lanes], 1, 0))
            rows = rows_s[u, q].astype(F32)
            out = rows + jnp.concatenate(mixed, axis=1)
            o_s[u, q] = out
            own = own + lane_sum(out * out)
            hit = hit + lane_sum(out * follow_of(rows))
            high = out.astype(BF16)
            low = (out - high.astype(F32)).astype(BF16)
            cands = cand_s[u, q]
            neg = neg + mm(high, cands, 1, 1) + mm(low, cands, 1, 1)
        stats = neg + jnp.where(col_id == CAND, own, 0.0) + jnp.where(col_id == CAND + 1, hit, 0.0)
        st_r[t, u] = stats.astype(BF16)
        for j in (2, 1, 3):
            st_copy(u, j).start()
        return carry

    lax.fori_loop(0, 4, forward_user, 0)

    def backward_user(u, carry):
        for j in (1, 3, 2):
            st_from(u, j).wait_recv()
        hot32 = hist_hot(u)
        hot_c32 = cand_hot(u)
        hot = hot32.astype(BF16)
        hot_c = hot_c32.astype(BF16)
        stats = (
            st_r[0, u].astype(F32) + st_r[1, u].astype(F32)
            + st_r[2, u].astype(F32) + st_r[3, u].astype(F32)
        )
        is_cand = col_id < CAND
        neg = jnp.where(is_cand, stats, 0.0)
        own = lane_sum(jnp.where(col_id == CAND, stats, 0.0))
        hit = lane_sum(jnp.where(col_id == CAND + 1, stats, 0.0))
        sq_rows = ssx[0] + ssx[1] + ssx[2] + ssx[3]
        sq_follow = pltpu.roll(mm(hot32, sqm[...], 0, 0, HI), HIST - 1, 0)
        sq_cand = mm(sq_rows, hot_c32, 1, 0, HI)[0:1]
        rn = lax.rsqrt(own + EPS)
        rf = lax.rsqrt(sq_follow + EPS)[:, 0:1]
        rc = lax.rsqrt(sq_cand + EPS)
        tl = SOFT * hit * rn * rf
        nl = SOFT * neg * rn * rc
        en = jnp.where(is_cand, jnp.exp(nl), 0.0)
        et = jnp.exp(tl)
        whole = et + lane_sum(en)
        span = len_ref[u] - 1
        over = 1.0 / (jnp.full((HIST, 1), 0, jnp.int32) + span).astype(F32)
        valid = iota((HIST, 1), 0) < span
        terms = jnp.where(valid, (jnp.log(whole) - tl) * over, 0.0)
        loss_ref[u] = jnp.broadcast_to(jnp.sum(terms, axis=0, keepdims=True), (1, HIST))
        g = jnp.where(valid, float(D) * over, 0.0)
        dtl = g * (et / whole - 1.0)
        dnl = (g / whole) * en
        dhit = dtl * (SOFT * rn * rf)
        dneg = dnl * (SOFT * rn * rc)
        down = -0.5 * rn * rn * (dtl * tl + lane_sum(dnl * nl))
        dsqf = -0.5 * dtl * tl * rf * rf
        dsqc = -0.5 * rc * rc * jnp.sum(dnl * nl, axis=0, keepdims=True)
        gsq[...] += mm(
            hot32, pltpu.roll(jnp.broadcast_to(dsqf, (HIST, HIST)), 1, 0), 1, 0, HI
        ) + lane_sum(hot_c32 * dsqc)
        dneg_low = dneg.astype(BF16)
        for q in range(4):
            out = o_s[u, q]
            rows = rows_s[u, q].astype(F32)
            dout = (
                2.0 * down * out + dhit * follow_of(rows) + mm(dneg_low, cand_s[u, q], 1, 0)
            )
            dcand = mm(dneg_low, out.astype(BF16), 0, 0).astype(BF16)
            drows = (dout + pltpu.roll(dhit * out, 1, 0)).astype(BF16)
            ae[q] += mm(hot, drows, 1, 0) + mm(hot_c, dcand, 1, 0)
            qn = qn_s[u, q]
            kn = kn_s[u, q]
            val = v_s[u, q]
            dout_low = dout.astype(BF16)
            dqs, dks, dvs = [], [], []
            for par in range(2):
                lanes = slice(par * HD, (par + 1) * HD)
                weights = w_s[u, 2 * q + par]
                wide = weights.astype(F32)
                dw = mm(dout_low[:, lanes], val[:, lanes], 1, 1)
                ds = (wide * (dw - lane_sum(dw * wide)) * scale).astype(BF16)
                dqs.append(mm(ds, kn[:, lanes], 1, 0))
                dks.append(mm(ds, qn[:, lanes], 0, 0))
                dvs.append(mm(weights, dout_low[:, lanes], 0, 0))
            aq[q] += mm(hot, jnp.concatenate(dqs, axis=1).astype(BF16), 1, 0)
            ak[q] += mm(hot, jnp.concatenate(dks, axis=1).astype(BF16), 1, 0)
            av[q] += mm(hot, jnp.concatenate(dvs, axis=1).astype(BF16), 1, 0)
        return carry

    lax.fori_loop(0, 4, backward_user, 0)

    for q in range(4):
        dqo[q] = aq[q].astype(BF16)
    to_groups(2, dqo, rq)
    rs = lax.rsqrt(sqm[...] * (1.0 / D) + EPS)[:, 0:1]
    part = jnp.zeros((8, 256), F32)
    for q in range(4):
        dn = av[q] + norm_heads_back(nrm[q].astype(F32), ak[q])
        rows = bufe[q].astype(F32)
        dn = dn * gain_of(q)
        part = part + mm(ones_q, dn * rows, 1, 1, HI)
        av[q] = dn
    nbx[t] = part
    own_nbx = lambda peer: nbx.at[t]
    start3(x_copy, 3, own_nbx, nbx)
    wait_in(x_from, 3, own_nbx, nbx)
    nb = columns(nbx[0] + nbx[1] + nbx[2] + nbx[3])[:, 0:1]
    slot_term = 2.0 * (gsq[...][:, 0:1] - (0.5 / D) * rs * rs * rs * nb)
    for q in range(4):
        eo[q] = (ae[q] + av[q] * rs + bufe[q].astype(F32) * slot_term).astype(BF16)
    to_groups(3, eo, re)

    all_in(2, rq)
    dq_item = norm_heads_back(q32[...], mm(gt[...], rq[...], 1, 0))
    dqg[t] = dq_item.astype(BF16)
    own_dqg = lambda peer: dqg.at[t]
    start3(x_copy, 4, own_dqg, dqg)
    wait_in(x_from, 4, own_dqg, dqg)
    gws_of = lambda peer: gws.at[peer]
    acc = jnp.zeros((256, 1024), F32)
    for tt in range(NT):
        acc = acc + mm(dqg[tt], wt[2 * tt : 2 * tt + 2].reshape(256, 1024), 1, 0)
    gws[...] = acc.astype(BF16).reshape(4, 64, 1024)
    start3(y_copy, 2, gws_of, gwr)
    gwr[y] = gws[y]
    all_in(3, re)
    es[...] = mm(gt[...], re[...], 1, 0).reshape(4, 64, 256)
    es_of = lambda peer: es.at[peer]
    start3(y_copy, 3, es_of, er)
    er[y] = es[y]

    wait_in(y_from, 2, gws_of, gwr)
    gw = (
        gwr[0].astype(F32) + gwr[1].astype(F32) + gwr[2].astype(F32) + gwr[3].astype(F32)
    ) * gu
    mine = pl.ds(pl.multiple_of(y * 64, 64), 64)
    emb = (hidden_ref[...].astype(F32) * rcol[mine, 0:1] * gi).astype(BF16).astype(F32)
    prod = gw * emb
    nwx[t] = mm(ones, jnp.concatenate([prod, prod], axis=0), 1, 1, HI)
    own_nwx = lambda peer: nwx.at[t]
    start3(x_copy, 5, own_nwx, nwx)
    wait_in(y_from, 3, es_of, er)
    wait_in(x_from, 5, own_nwx, nwx)
    nw = columns(nwx[0] + nwx[1] + nwx[2] + nwx[3])[0:64, 0:1]
    rs_own = rscol[mine, 0:1]
    coef = (-1.0 / D) * rs_own * rs_own * rs_own * nw
    for h in range(8):
        lanes = slice(h * HD, (h + 1) * HD)
        par, q = h // 4, h % 4
        grad_ref[:, lanes] = (
            er[q][:, par * HD : (par + 1) * HD] + gw[:, lanes] * rs_own + emb[:, lanes] * coef
        )

    wait_out(y_copy, 0, own_hd, hd)
    wait_out(y_copy, 1, own_sel, selb)
    wait_out(y_copy, 2, gws_of, gwr)
    wait_out(y_copy, 3, es_of, er)
    wait_out(x_copy, 0, own_sqx, sqx)
    wait_out(x_copy, 1, ps_of, pr)
    wait_out(x_copy, 2, own_ssx, ssx)
    wait_out(x_copy, 3, own_nbx, nbx)
    wait_out(x_copy, 4, own_dqg, dqg)
    wait_out(x_copy, 5, own_nwx, nwx)
    for u in range(4):
        for j in (1, 3, 2):
            st_copy(u, j).wait_send()
    for stream in range(4):
        for step in range(RING[stream]):
            ring(stream, step).wait_send()
    for b in range(NZ):
        for half in range(2):
            partner(b, c, half).wait_send()
    for k, flat in ((0, oute), (1, outq), (2, rq), (3, re)):
        all_out(k, flat)


def local(item_hidden, item_gain, send_item, pos_slot, hist_len, user_gain, query_weight):
    me = lax.axis_index("sect")
    y = (me // 2) % 4
    picks = jnp.where(send_item[0] < 0, -1, send_item[0] + y * 64)
    sel = jnp.where(
        (jnp.arange(4) == y)[None, :, None], picks[:, None, :], -1
    ).reshape(1, 1024).astype(jnp.int32)
    owner, slot = pos_slot // 4, pos_slot % 4
    place = ((owner // 8 * 2 + owner % 2) * 4 + owner // 2 % 4) * 4 + slot
    cand = jnp.pad(place[:, HIST:], ((0, 0), (0, HIST - CAND)), constant_values=-1)
    pos = jnp.concatenate([place[:, :HIST], cand], axis=0).reshape(8, 1, HIST).astype(jnp.int32)
    vmem = pltpu.VMEM
    dma = pltpu.SemaphoreType.DMA
    quarter = lambda kind: vmem((4, 256, 256), kind)
    user = lambda kind: vmem((4, 4, HIST, 256), kind)
    grad, loss = pl.pallas_call(
        kernel,
        out_shape=(
            jax.ShapeDtypeStruct((64, 1024), F32),
            jax.ShapeDtypeStruct((4, 1, HIST), F32),
        ),
        in_specs=[pl.BlockSpec(memory_space=pltpu.SMEM)]
        + [pl.BlockSpec(memory_space=pltpu.VMEM)] * 6,
        out_specs=(
            pl.BlockSpec(memory_space=pltpu.VMEM),
            pl.BlockSpec(memory_space=pltpu.VMEM),
        ),
        scratch_shapes=[
            vmem((4, 64, 1024), BF16),
            vmem((4, 1, 1024), jnp.int32),
            vmem((8, 2, 64, 1024), BF16),
            vmem((4, 16, 256), F32),
            quarter(BF16),
            quarter(BF16),
            vmem((1024, 256), BF16),
            vmem((1024, 256), BF16),
            quarter(BF16),
            quarter(BF16),
            vmem((256, 1024), BF16),
            quarter(BF16),
            quarter(BF16),
            vmem((4, 8, 256), F32),
            vmem((256, HIST), F32),
            vmem((256, 256), F32),
            vmem((256, HIST), F32),
            vmem((256, HIST), F32),
            user(BF16),
            user(BF16),
            user(BF16),
            user(BF16),
            user(BF16),
            vmem((4, 8, HIST, HIST), BF16),
            user(F32),
            vmem((4, 4, HIST, HIST), BF16),
            quarter(F32),
            quarter(F32),
            quarter(F32),
            quarter(F32),
            vmem((256, HIST), F32),
            quarter(BF16),
            quarter(BF16),
            vmem((1024, 256), BF16),
            vmem((1024, 256), BF16),
            quarter(BF16),
            vmem((4, 64, 1024), BF16),
            vmem((4, 64, 1024), BF16),
            vmem((4, 64, 256), F32),
            vmem((4, 64, 256), F32),
            vmem((4, 8, 256), F32),
            vmem((4, 8, HIST), F32),
            dma((12, 4)),
            dma((12, 4)),
            dma((4, 4)),
            dma((4, 4)),
            dma((4, 4)),
            dma((4, 4)),
            dma((8, 2)),
            dma((8, 2)),
            dma((4,)),
            dma((4,)),
        ],
        compiler_params=pltpu.CompilerParams(
            collective_id=0, has_side_effects=True, vmem_limit_bytes=60 * 1024 * 1024
        ),
    )(
        hist_len, item_hidden, query_weight, item_gain.reshape(1, 1024),
        user_gain.reshape(1, 1024), sel, pos,
    )
    return (grad, loss[:, 0, 0])


def solution(mesh):
    placed = (
        P("sect", "tp"),
        P("tp"),
        P("sect", None, None),
        P("sect", None),
        P("sect"),
        P("tp"),
        P("tp", "sect"),
    )
    return jax.shard_map(
        local, mesh=mesh, in_specs=placed, out_specs=(P("sect", "tp"), P("sect")), check_vma=False
    )
```

time: 339 us -> 138 us (0.41)
  Pallas kernels: 0 us -> 128 us
  waiting for transfers between devices: 112 us -> 0 us
  other arithmetic: 61.6 us -> 0.73 us
  local copies, waits for them, and re-layouts: 50 us -> 6.72 us
  matrix products: 37 us -> 0 us
  blocking collectives: 30.5 us -> 0 us
  starting transfers between devices: 27.5 us -> 0 us
  between operations: 14.6 us -> 0.73 us
    pallas_call x0 -> x1, Pallas kernels: none -> 128 us  [local(): pl.pallas_call(kernel, out_shape=(jax.ShapeDtypeStruct((64, 1024), F32),...]
    all_gather x2 -> x0, waiting for transfers between devices: 40.5 us -> none  [the longest x1 34.8 us: local(): lax.all_gather(query_weight, 'sect', axis=1, tiled=True)]
    dot_general x11 -> x0, matrix products: 37 us -> none  [the longest x3 8.19 us: attend(): jnp.einsum('uihd,ujhd->uhij', query_heads, key_heads, preferred_element_t...]
    all_to_all x2 -> x0, waiting for transfers between devices: 36.3 us -> none  [the longest x1 19.4 us: local(): lax.all_to_all(outgoing, 'sect', split_axis=0, concat_axis=0, tiled=True)]
    scatter-add x7 -> x0, other arithmetic: 35.3 us -> none  [the longest x6 32.6 us: segment_rows(): jax.ops.segment_sum(values.reshape((-1,) + values.shape[2:]), places.resh...]
    psum x1 -> x0, waiting for transfers between devices: 34.6 us -> none  [local(): lax.psum(partial_stats[2].astype(jnp.bfloat16), 'tp').astype(jnp.float32)]
    psum x4 -> x0, blocking collectives: 30.5 us -> none  [the longest x1 9.29 us: local(): item_squares = lax.psum(jnp.sum(hidden * hidden, axis=1), 'tp')]
    all_to_all x2 -> x0, starting transfers between devices: 27.2 us -> none  [the longest x1 14.3 us: local(): lax.all_to_all(outgoing, 'sect', split_axis=0, concat_axis=0, tiled=True)]
  transfers between devices with their start and end apart: 6 -> 0, of which waited for: 5 -> 0; matrix products, arithmetic and copies ran while one was open for 20% -> 0% of each run, Pallas kernels for 0% -> 0%
where the time goes in v1:
time: 138 us; the launch traced here: 136 us
  Pallas kernels  128 us (93%)
  local copies, waits for them, and re-layouts  6.72 us (5%)
    pallas_call x1, Pallas kernels, local(): pl.pallas_call(kernel, out_shape=(jax.ShapeDtypeStruct((64, 1024), F32),...  128 us
    unnamed x14, local copies, waits for them, and re-layouts  4.05 us

profile of v1, /device:TPU:1, one launch (start us, length us, event | category | flops | bytes accessed | tf_op | source)
XLA Modules:
  0.0 135.8 jit_solution(620758748884707513)
XLA Ops:
  0.7 0.0 copy-start.5
  0.7 0.0 copy-start.1
  0.7 0.6 copy-done.5
  1.3 0.0 copy-done.1
  1.4 0.0 copy-start.2
  1.4 0.6 select_add_fusion
  2.0 0.1 copy-done.2
  2.1 0.0 copy-start.3
  2.1 0.6 reshape.57.gi_ref
  2.7 0.1 copy-done.3
  2.8 0.6 reshape.58.gu_ref
  3.4 0.1 copy.11
  3.5 0.0 copy-start
  3.5 0.1 broadcast_select_fusion
  3.6 0.8 select_n.66.sel_ref
  4.3 0.0 copy-done
  4.4 0.8 copy.12.w_ref
  5.2 127.6 %shard_map.86 = (f32[64,1024]{1,0:T(8,128)}, f32[4,1,128]{2,1,0:T(1,128)}) custom-call(s32[4]{0:T(128)} %len_ref.1, bf16[64,1024]{1,0:T(8,128)(2,1)} %hidden_ref.1, bf16[1024,64]{1,0:T(8,128)(2,1)} %copy.12.w_ref, bf16[1,1024]{1,0:T(2,128)(2,1)} %reshape.57.gi_ref, bf16[1,1024]{1,0:T(2,128)(2,1)} %reshape.58.gu_ref, s32[1,1024]{1,0:T(1,128)} %select_n.66.sel_ref, ...), custom_call_target="tpu_custom_call" | custom-call | tf_op jit(solution)/shard_map/pallas_call | solution.py:539
  132.9 0.0 copy-start.4
  132.9 0.6 copy-done.4
  133.5 0.6 slice_reduce_fusion
  134.1 1.7 %copy.14 = f32[64,1024]{1,0:T(8,128)} copy(f32[64,1024]{1,0:T(8,128)} %get-tuple-element.8) | data formatting | bytes 524288
  (5 shorter events, 0.0 us)
Async XLA Ops:
  0.7 0.7 copy-start.5
  0.7 0.7 copy-start.1
  1.4 0.7 copy-start.2
  2.1 0.7 copy-start.3
  3.5 0.9 copy-start
  132.9 0.7 copy-start.4

commit v2 on v1

v2 whole, which is shorter than its diff:
```python
import jax
import jax.numpy as jnp
from jax import lax
from jax.experimental import pallas as pl
from jax.experimental.pallas import tpu as pltpu
from jax.sharding import PartitionSpec as P

D = 4096
HD = 128
HIST = 128
CAND = 64
NZ, NY, NT = 8, 4, 4
NS = 64
EPS = 1e-06
SOFT = 20.0
F32, BF16 = jnp.float32, jnp.bfloat16
MESH = pl.DeviceIdType.MESH
RING = (4, 3, 3, 4)


def mm(a, b, ca, cb, precision=None):
    return lax.dot_general(
        a, b, (((ca,), (cb,)), ((), ())), preferred_element_type=F32, precision=precision
    )


def split3(values):
    high = values.astype(BF16)
    rest = values - high.astype(F32)
    mid = rest.astype(BF16)
    return high, mid, (rest - mid.astype(F32)).astype(BF16)


def row_parts(row):
    parts = split3(jnp.broadcast_to(row, (8, row.shape[1])))
    index = iota((8, row.shape[1]), 0)
    out = jnp.where(index == 0, parts[0].astype(F32), 0.0)
    out = jnp.where(index == 1, parts[1].astype(F32), out)
    return jnp.where(index == 2, parts[2].astype(F32), out).astype(BF16)


def lane_parts(values):
    parts = split3(values)
    index = iota(values.shape, 1)
    out = jnp.where(index == 0, parts[0].astype(F32), 0.0)
    out = jnp.where(index == 1, parts[1].astype(F32), out)
    return jnp.where(index == 2, parts[2].astype(F32), out).astype(BF16)


def columns(row):
    return mm(row_parts(row), jnp.ones((8, 128), BF16), 0, 0)


def row_sums(values):
    ones = jnp.ones((8, values.shape[1]), BF16)
    high, mid, low = split3(values)
    return mm(ones, high, 1, 1) + mm(ones, mid, 1, 1) + mm(ones, low, 1, 1)


def lane_sum(values):
    return jnp.sum(values, axis=1, keepdims=True)


def iota(shape, dim):
    return lax.broadcasted_iota(jnp.int32, shape, dim)


def one_hot(row, count):
    return jnp.where(iota((count, row.shape[1]), 0) == row, 1.0, 0.0)


def norm_heads(values):
    heads, roots = [], []
    for par in range(2):
        part = values[:, par * HD : (par + 1) * HD]
        root = lax.rsqrt(lane_sum(part * part) * (1.0 / HD) + EPS)
        heads.append(part * root)
        roots.append(root)
    return heads, roots


def norm_heads_back(values, grads):
    heads, roots = norm_heads(values)
    out = []
    for par in range(2):
        grad = grads[:, par * HD : (par + 1) * HD]
        out.append(
            roots[par] * (grad - heads[par] * (lane_sum(grad * heads[par]) * (1.0 / HD)))
        )
    return jnp.concatenate(out, axis=1)


def kernel(
    len_ref, hidden_ref, w_ref, gi_ref, gu_ref, send_ref, pos_ref,
    grad_ref, loss_ref,
    hd, selb, wt, sqx, ps, pr, oute, outq, bufe, bufq, gt, nrm, knb, ssx, sqm, q32,
    rcol, rscol, pos_s, hot, hott, sqf_s, sqc_s,
    rc_s, kn_s, v_s, qn_s, w_s, o_s, st_r, dsc, dneg_s, gfol, grow,
    av, ae, dqo, eo, rq, re, dqg, gws, gwr, es, er, nbx, sdx, sdy,
    xs, xr, ys, yr, ring_s, ring_r, par_s, par_r, a2a_s, a2a_r,
):
    me = lax.axis_index("sect")
    t = lax.axis_index("tp")
    z, y, c = me // 8, (me // 2) % 4, me % 2
    blk = z * 2 + c

    def send(src, dst, ssem, rsem, sect, tp):
        return pltpu.make_async_remote_copy(
            src_ref=src, dst_ref=dst, send_sem=ssem, recv_sem=rsem,
            device_id=(sect, tp), device_id_type=MESH,
        )

    def sect_of(zz, yy, cc):
        return zz * 8 + yy * 2 + cc

    def x_copy(k, src, dst, j):
        peer = (t + j) % NT
        return send(src(peer), dst.at[t], xs.at[k, peer], xr.at[k, t], me, peer)

    def x_from(k, src, dst, j):
        sender = (t + NT - j) % NT
        return send(src(t), dst.at[sender], xs.at[k, sender], xr.at[k, sender], me, sender)

    def y_copy(k, src, dst, j):
        peer = (y + j) % NY
        return send(src(peer), dst.at[y], ys.at[k, peer], yr.at[k, y], sect_of(z, peer, c), t)

    def y_from(k, src, dst, j):
        sender = (y + NY - j) % NY
        return send(
            src(y), dst.at[sender], ys.at[k, sender], yr.at[k, sender], sect_of(z, sender, c), t
        )

    def start3(copy, k, src, dst):
        for j in (2, 1, 3):
            copy(k, src, dst, j).start()

    def wait_in(came, k, src, dst):
        for j in (1, 3, 2):
            came(k, src, dst, j).wait_recv()

    def wait_out(copy, k, src, dst):
        for j in (1, 3, 2):
            copy(k, src, dst, j).wait_send()

    def rows_of(first):
        return pl.ds(pl.multiple_of(first * 16, 16), 16)

    def to_readers(k, out, buf, lanes):
        pltpu.make_async_copy(
            out.at[rows_of(me), lanes], buf.at[y, rows_of(blk), lanes], a2a_r.at[k]
        ).start()

        def step(j, carry):
            peer = (me + j) % NS
            send(
                out.at[rows_of(peer), lanes], buf.at[y, rows_of(blk), lanes],
                a2a_s.at[k], a2a_r.at[k], peer, t,
            ).start()
            return carry

        lax.fori_loop(1, NS, step, 0)

    def to_group(k, out, buf, group, same):
        def copy(j):
            b = (blk + j) % 16
            return send(
                out.at[group, rows_of(b)], buf.at[rows_of(me)],
                a2a_s.at[k], a2a_r.at[k], sect_of(b // 2, group, b % 2), t,
            )

        @pl.when(same)
        def _():
            pltpu.make_async_copy(
                out.at[group, rows_of(blk)], buf.at[rows_of(me)], a2a_r.at[k]
            ).start()

        @pl.when(jnp.logical_not(same))
        def _():
            copy(0).start()

        def step(j, carry):
            copy(j).start()
            return carry

        lax.fori_loop(1, 16, step, 0)

    def all_in(k, view):
        pltpu.make_async_copy(view, view, a2a_r.at[k]).wait()

    def all_out(k, view):
        pltpu.make_async_copy(view, view, a2a_s.at[k]).wait()

    def ring(stream, step):
        way = 1 if stream < 2 else NZ - 1
        block = (z + (NZ - way) * step) % NZ
        part = wt.at[block, c, pl.ds((stream % 2) * 32, 32)]
        return send(
            part, part, ring_s.at[stream, step], ring_r.at[stream, step],
            sect_of((z + way) % NZ, y, c), t,
        )

    def ring_from(stream, step):
        way = 1 if stream < 2 else NZ - 1
        block = (z + (NZ - way) * (step + 1)) % NZ
        part = wt.at[block, c, pl.ds((stream % 2) * 32, 32)]
        return block, send(
            part, part, ring_s.at[stream, step], ring_r.at[stream, step],
            sect_of((z + way) % NZ, y, c), t,
        )

    def partner(block, core, half):
        part = wt.at[block, core, pl.ds(half * 32, 32)]
        return send(
            part, part, par_s.at[block, half], par_r.at[block, half], sect_of(z, y, 1 - c), t
        )

    def partner_in(block, half):
        partner(block, 1 - c, half).wait_recv()

    def advance(step):
        for stream in (0, 2, 1, 3):
            if step >= RING[stream]:
                continue
            block, came = ring_from(stream, step)
            came.wait_recv()
            if step + 1 < RING[stream]:
                ring(stream, step + 1).start()
            partner(block, c, stream % 2).start()

    barrier = pltpu.get_barrier_semaphore()
    for j in range(1, 8):
        pl.semaphore_signal(
            barrier, inc=1, device_id=(z * 8 + (me + j) % 8, t), device_id_type=MESH
        )
    for j in (1, NZ - 1):
        pl.semaphore_signal(
            barrier, inc=1, device_id=(sect_of((z + j) % NZ, y, c), t), device_id_type=MESH
        )
    for j in range(1, NT):
        pl.semaphore_signal(barrier, inc=1, device_id=(me, (t + j) % NT), device_id_type=MESH)

    hd[y] = hidden_ref[...]
    wt[z, c] = w_ref[...]
    spread = jnp.where((iota((64, 1024), 1) >> 4) == iota((64, 1024), 0), 1.0, 0.0).astype(BF16)
    named = mm(send_ref[...].astype(F32).astype(BF16), spread, 1, 0)
    lane = iota((1, 1024), 1)
    pick = jnp.full((1, 1024), -1.0, F32)
    for s in range(4):
        pick = jnp.where((lane & 3) == s, named[s : s + 1], pick)
    base = (jnp.zeros((1, 1024), jnp.int32) + y * 64).astype(F32)
    selb[y] = jnp.where((((lane >> 2) & 3) == y) & (pick >= 0.0), pick + base, -1.0)
    pl.semaphore_wait(barrier, 7 + 2 + NT - 1)

    own_hd = lambda peer: hd.at[y]
    own_sel = lambda peer: selb.at[y]
    for stream in (0, 2, 1, 3):
        ring(stream, 0).start()
    start3(y_copy, 0, own_hd, hd)
    start3(y_copy, 1, own_sel, selb)
    for half in range(2):
        partner(z, c, half).start()

    slots = pos_ref[...]
    owner = slots >> 2
    pos_s[...] = jnp.full(pos_s.shape, -1, jnp.int32)
    pos_s[:, 0 : HIST + CAND] = (
        ((owner >> 3) << 5) | ((owner & 1) << 4) | (((owner >> 1) & 3) << 2) | (slots & 3)
    )
    for u in range(4):
        for kind in range(2):
            row = pos_s[u : u + 1, kind * HIST : (kind + 1) * HIST]
            picked = one_hot(row, 256)
            first = (4 * kind + u) * HIST
            hot[:, first : first + HIST] = picked.astype(BF16)
            hott[first : first + HIST, :] = jnp.transpose(picked).astype(BF16)

    advance(0)
    wait_in(y_from, 0, own_hd, hd)
    gi = gi_ref[...].astype(F32).reshape(1, 1024)
    gu = gu_ref[...].astype(F32).reshape(1, 1024)
    lhs = (hd[...].reshape(256, 1024).astype(F32) * (gi * gu)).astype(BF16)

    near = z // 2
    turn = 2 * (z % 2) - 1
    order = (near, (near + turn + NT) % NT, (near - turn + NT) % NT, (near + 2) % NT)

    def ps_copy(peer):
        return send(ps.at[peer], pr.at[t], xs.at[1, peer], xr.at[1, t], me, peer)

    def project(index):
        part = order[index]
        block = wt[pl.ds(2 * part, 2)].reshape(256, 1024)
        ps[part] = mm(lhs, block, 1, 1).astype(BF16)

        @pl.when(part != t)
        def _():
            ps_copy(part).start()

    def partners_in(step):
        if step == 0:
            for half in range(2):
                partner_in(z, half)
        for stream in range(4):
            if step < RING[stream]:
                way = 1 if stream < 2 else NZ - 1
                partner_in((z + (NZ - way) * (step + 1)) % NZ, stream % 2)

    partners_in(0)
    project(0)
    hidden = hd[...].reshape(256, 1024).astype(F32)
    sqx[t, pl.ds(0, 8), :] = row_sums(hidden * hidden)
    gained = hidden * gi
    sqx[t, pl.ds(8, 8), :] = row_sums(gained * gained)
    own_sqx = lambda peer: sqx.at[t]
    start3(x_copy, 0, own_sqx, sqx)
    advance(1)
    partners_in(1)
    project(1)
    wait_in(y_from, 1, own_sel, selb)
    picks = jnp.maximum(jnp.maximum(selb[0], selb[1]), jnp.maximum(selb[2], selb[3]))
    gt[...] = one_hot(picks.astype(jnp.int32), 256).astype(BF16)
    advance(2)
    partners_in(2)
    project(2)
    wait_in(x_from, 0, own_sqx, sqx)
    sums = sqx[0] + sqx[1] + sqx[2] + sqx[3]
    r_row = lax.rsqrt(sums[0:1] * (1.0 / D) + EPS)
    rs_row = lax.rsqrt(r_row * r_row * sums[8:9] * (1.0 / D) + EPS)
    rcol[...] = columns(r_row)
    rscol[...] = columns(rs_row)
    pieces = []
    for par in range(2):
        head = par * 4 + y
        lanes = pl.ds(pl.multiple_of(head * HD, HD), HD)
        piece = hd[:, :, lanes].reshape(256, HD).astype(F32)
        gain = jnp.zeros((1, HD), F32)
        for h in range(8):
            gain = gain + jnp.where(head == h, gi[:, h * HD : (h + 1) * HD], 0.0)
        pieces.append((piece * rcol[...] * gain).astype(BF16))
    oute[...] = mm(gt[...], jnp.concatenate(pieces, axis=1), 0, 0).astype(BF16)
    advance(3)
    partners_in(3)
    project(3)
    both = slice(0, 256)
    to_readers(0, oute, bufe, both)
    pr[t] = ps[t]
    for j in (1, 3, 2):
        sender = (t + j) % NT
        send(
            ps.at[t], pr.at[sender], xs.at[1, sender], xr.at[1, sender], me, sender
        ).wait_recv()
    total = (
        pr[0].astype(F32) + pr[1].astype(F32) + pr[2].astype(F32) + pr[3].astype(F32)
    ) * (rcol[...] * rscol[...])[:, 0:1]
    q32[...] = total
    heads, _ = norm_heads(total)
    outq[...] = mm(gt[...], jnp.concatenate(heads, axis=1).astype(BF16), 0, 0).astype(BF16)
    halves = (slice(0, HD), slice(HD, 2 * HD))
    to_readers(1, outq, bufq, halves[0])
    to_readers(4, outq, bufq, halves[1])

    all_in(0, bufe)
    part = jnp.zeros((8, 256), F32)
    for q in range(4):
        rows = bufe[q].astype(F32)
        part = part + row_sums(rows * rows)
    ssx[t] = part
    own_ssx = lambda peer: ssx.at[t]
    start3(x_copy, 2, own_ssx, ssx)
    for q in range(4):
        rc_s[q] = mm(hott[...], bufe[q], 1, 0).astype(BF16)

    def gain_of(q):
        return jnp.concatenate(
            [gu[:, q * HD : (q + 1) * HD], gu[:, (4 + q) * HD : (5 + q) * HD]], axis=1
        )

    wait_in(x_from, 2, own_ssx, ssx)
    sq_row = (ssx[0] + ssx[1] + ssx[2] + ssx[3])[0:1]
    sqm[...] = columns(sq_row)
    rs = lax.rsqrt(sqm[...] * (1.0 / D) + EPS)[:, 0:1]
    for q in range(4):
        low = (bufe[q].astype(F32) * rs * gain_of(q)).astype(BF16)
        nrm[q] = low
        heads, _ = norm_heads(low.astype(F32))
        knb[q] = jnp.concatenate(heads, axis=1).astype(BF16)
    for q in range(4):
        kn_s[q] = mm(hott[0:512], knb[q], 1, 0).astype(BF16)
        v_s[q] = mm(hott[0:512], nrm[q], 1, 0).astype(BF16)
    sqf_s[...] = jnp.broadcast_to(
        lane_sum(mm(hott[0:512], lane_parts(sqm[...]), 1, 0)), (512, HIST)
    )
    sqc = jnp.sum(mm(row_parts(sq_row), hot[:, 512:1024], 1, 0), axis=0, keepdims=True)
    for u in range(4):
        sqc_s[u] = sqc[:, u * HIST : (u + 1) * HIST]

    scale = HD ** (-0.5)
    row_id = iota((HIST, HIST), 0)
    col_id = iota((HIST, HIST), 1)

    def follow_of(rows):
        moved = pltpu.roll(rows, HIST - 1, 0)
        return jnp.where(iota(rows.shape, 0) < HIST - 1, moved, 0.0)

    def st_copy(u, j):
        peer = (t + j) % NT
        return send(st_r.at[t, u], st_r.at[t, u], xs.at[6 + u, peer], xr.at[6 + u, t], me, peer)

    def st_from(u, j):
        sender = (t + NT - j) % NT
        return send(
            st_r.at[t, u], st_r.at[sender, u], xs.at[6 + u, sender], xr.at[6 + u, sender],
            me, sender,
        )

    def user_rows(u):
        return pl.ds(pl.multiple_of(u * HIST, HIST), HIST)

    def attend(u, par):
        span = user_rows(u)
        lanes = halves[par]
        mask = jnp.where((col_id <= row_id) & (col_id < len_ref[u]), 1.0, 0.0)
        for q in range(4):
            weights = jnp.exp(mm(qn_s[q, span, lanes], kn_s[q, span, lanes], 1, 1) * scale) * mask
            weights = (weights * (1.0 / lane_sum(weights))).astype(BF16)
            w_s[2 * q + par, span] = weights
            o_s[q, span, lanes] = rc_s[q, span, lanes].astype(F32) + mm(
                weights, v_s[q, span, lanes], 1, 0
            )

    def first_half(u, carry):
        attend(u, 0)
        return carry

    def second_half(u, carry):
        attend(u, 1)
        span = user_rows(u)
        cspan = user_rows(u + 4)
        own = jnp.zeros((HIST, 1), F32)
        hit = jnp.zeros((HIST, 1), F32)
        neg = jnp.zeros((HIST, HIST), F32)
        for q in range(4):
            out = o_s[q, span]
            own = own + lane_sum(out * out)
            hit = hit + lane_sum(out * follow_of(rc_s[q, span].astype(F32)))
            high = out.astype(BF16)
            low = (out - high.astype(F32)).astype(BF16)
            cands = rc_s[q, cspan]
            neg = neg + mm(high, cands, 1, 1) + mm(low, cands, 1, 1)
        stats = neg + jnp.where(col_id == CAND, own, 0.0) + jnp.where(col_id == CAND + 1, hit, 0.0)
        st_r[t, u] = stats.astype(BF16)
        for j in (2, 1, 3):
            st_copy(u, j).start()
        return carry

    for par, step in ((0, first_half), (1, second_half)):
        all_in(1 if par == 0 else 4, outq.at[:, halves[0]])
        for q in range(4):
            qn_s[q, :, halves[par]] = mm(hott[0:512], bufq[q, :, halves[par]], 1, 0).astype(BF16)
        lax.fori_loop(0, 4, step, 0)

    def losses(u, carry):
        for j in (1, 3, 2):
            st_from(u, j).wait_recv()
        stats = (
            st_r[0, u].astype(F32) + st_r[1, u].astype(F32)
            + st_r[2, u].astype(F32) + st_r[3, u].astype(F32)
        )
        is_cand = col_id < CAND
        neg = jnp.where(is_cand, stats, 0.0)
        own = lane_sum(jnp.where(col_id == CAND, stats, 0.0))
        hit = lane_sum(jnp.where(col_id == CAND + 1, stats, 0.0))
        sq_follow = pltpu.roll(sqf_s[user_rows(u)], HIST - 1, 0)[:, 0:1]
        rn = lax.rsqrt(own + EPS)
        rf = lax.rsqrt(sq_follow + EPS)
        rc = lax.rsqrt(sqc_s[u] + EPS)
        tl = SOFT * hit * rn * rf
        nl = SOFT * neg * rn * rc
        en = jnp.where(is_cand, jnp.exp(nl), 0.0)
        et = jnp.exp(tl)
        whole = et + lane_sum(en)
        span = len_ref[u] - 1
        over = 1.0 / (jnp.full((HIST, 1), 0, jnp.int32) + span).astype(F32)
        valid = iota((HIST, 1), 0) < span
        terms = jnp.where(valid, (jnp.log(whole) - tl) * over, 0.0)
        loss_ref[u] = jnp.broadcast_to(jnp.sum(terms, axis=0, keepdims=True), (1, HIST))
        g = jnp.where(valid, float(D) * over, 0.0)
        dtl = g * (et / whole - 1.0)
        dnl = (g / whole) * en
        dsc[u, 0] = jnp.broadcast_to(
            -rn * rn * (dtl * tl + lane_sum(dnl * nl)), (HIST, HIST)
        )
        dsc[u, 1] = jnp.broadcast_to(dtl * (SOFT * rn * rf), (HIST, HIST))
        dneg_s[u] = (dnl * (SOFT * rn * rc)).astype(BF16)
        dsqf = jnp.broadcast_to(-0.5 * dtl * tl * rf * rf, (HIST, HIST))
        gfol[user_rows(u)] = pltpu.roll(dsqf, 1, 0)
        grow[u] = -0.5 * rc * rc * jnp.sum(dnl * nl, axis=0, keepdims=True)
        return carry

    lax.fori_loop(0, 4, losses, 0)

    def backward_quarter(i, carry):
        q = (y + 1 + i) % 4
        for u in range(4):
            span = slice(u * HIST, (u + 1) * HIST)
            cspan = slice((4 + u) * HIST, (5 + u) * HIST)
            twice_down = jnp.concatenate([dsc[u, 0]] * 2, axis=1)
            dhit = jnp.concatenate([dsc[u, 1]] * 2, axis=1)
            out = o_s[q, span]
            rows = rc_s[q, span].astype(F32)
            cands = rc_s[q, cspan]
            dneg = dneg_s[u]
            dout = twice_down * out + dhit * follow_of(rows) + mm(dneg, cands, 1, 0)
            rc_s[q, cspan] = mm(dneg, out.astype(BF16), 0, 0).astype(BF16)
            rc_s[q, span] = (dout + pltpu.roll(dhit * out, 1, 0)).astype(BF16)
            dout_low = dout.astype(BF16)
            for par in range(2):
                lanes = halves[par]
                qn = qn_s[q, span, lanes]
                kn = kn_s[q, span, lanes]
                grad = dout_low[:, lanes]
                weights = w_s[2 * q + par, span]
                wide = weights.astype(F32)
                dw = mm(grad, v_s[q, span, lanes], 1, 1)
                ds = (wide * (dw - lane_sum(dw * wide)) * scale).astype(BF16)
                qn_s[q, span, lanes] = mm(ds, kn, 1, 0).astype(BF16)
                kn_s[q, span, lanes] = mm(ds, qn, 0, 0).astype(BF16)
                v_s[q, span, lanes] = mm(weights, grad, 0, 0).astype(BF16)
        dqo[q] = mm(hot[:, 0:512], qn_s[q], 1, 0).astype(BF16)
        to_group(2, dqo, rq, q, i == 3)
        return carry

    lax.fori_loop(0, 4, backward_quarter, 0)

    rs = lax.rsqrt(sqm[...] * (1.0 / D) + EPS)[:, 0:1]
    part = jnp.zeros((8, 256), F32)
    for q in range(4):
        dk = mm(hot[:, 0:512], kn_s[q], 1, 0)
        dn = mm(hot[:, 0:512], v_s[q], 1, 0) + norm_heads_back(nrm[q].astype(F32), dk)
        dn = dn * gain_of(q)
        part = part + row_sums(dn * bufe[q].astype(F32))
        av[q] = dn
    nbx[t] = part
    own_nbx = lambda peer: nbx.at[t]
    start3(x_copy, 3, own_nbx, nbx)
    gsq = lane_sum(mm(hot[:, 0:512], lane_parts(gfol[...]), 1, 0)) + lane_sum(
        mm(
            hot[:, 512:1024],
            row_parts(jnp.concatenate([grow[u] for u in range(4)], axis=1)), 1, 1,
        )
    )
    for q in range(4):
        ae[q] = mm(hot[...], rc_s[q], 1, 0) + av[q] * rs
    wait_in(x_from, 3, own_nbx, nbx)
    nb = columns((nbx[0] + nbx[1] + nbx[2] + nbx[3])[0:1])[:, 0:1]
    slot_term = 2.0 * (gsq - (0.5 / D) * rs * rs * rs * nb)
    for q in range(4):
        eo[q] = (ae[q] + bufe[q].astype(F32) * slot_term).astype(BF16)

    all_in(2, rq)
    dq_item = norm_heads_back(q32[...], mm(gt[...], rq[...], 1, 0)).astype(BF16)
    dqg[t] = dq_item
    own_dqg = lambda peer: dqg.at[t]
    start3(x_copy, 4, own_dqg, dqg)
    sdx[t] = row_sums(dq_item.astype(F32) * q32[...])
    own_sdx = lambda peer: sdx.at[t]
    start3(x_copy, 5, own_sdx, sdx)

    def return_group(i, carry):
        group = (y + 1 + i) % 4
        to_group(3, eo, re, group, i == 3)
        return carry

    lax.fori_loop(0, 4, return_group, 0)
    wait_in(x_from, 4, own_dqg, dqg)
    gws_of = lambda peer: gws.at[peer]
    acc = jnp.zeros((256, 1024), F32)
    for tt in range(NT):
        acc = acc + mm(dqg[tt], wt[2 * tt : 2 * tt + 2].reshape(256, 1024), 1, 0)
    gws[...] = acc.astype(BF16).reshape(4, 64, 1024)
    start3(y_copy, 2, gws_of, gwr)
    gwr[y] = gws[y]
    wait_in(x_from, 5, own_sdx, sdx)
    sdy[y] = sdx[0] + sdx[1] + sdx[2] + sdx[3]
    own_sdy = lambda peer: sdy.at[y]
    start3(y_copy, 4, own_sdy, sdy)
    all_in(3, re)
    es[...] = mm(gt[...], re[...], 1, 0).reshape(4, 64, 256)
    es_of = lambda peer: es.at[peer]
    start3(y_copy, 3, es_of, er)
    er[y] = es[y]

    mine = pl.ds(pl.multiple_of(y * 64, 64), 64)
    emb = (hidden_ref[...].astype(F32) * rcol[mine, 0:1] * gi).astype(BF16).astype(F32)
    rs_own = rscol[mine, 0:1]
    wait_in(y_from, 4, own_sdy, sdy)
    sqm[...] = columns((sdy[0] + sdy[1] + sdy[2] + sdy[3])[0:1])
    coef = (-1.0 / D) * rs_own * rs_own * sqm[mine, 0:1]
    direct = emb * coef
    wait_in(y_from, 2, gws_of, gwr)
    gw = (
        gwr[0].astype(F32) + gwr[1].astype(F32) + gwr[2].astype(F32) + gwr[3].astype(F32)
    ) * gu * rs_own + direct
    wait_in(y_from, 3, es_of, er)
    for h in range(8):
        lanes = slice(h * HD, (h + 1) * HD)
        par, q = h // 4, h % 4
        grad_ref[:, lanes] = er[q][:, par * HD : (par + 1) * HD] + gw[:, lanes]

    for k, src, dst in (
        (0, own_hd, hd), (1, own_sel, selb), (2, gws_of, gwr), (3, es_of, er), (4, own_sdy, sdy)
    ):
        wait_out(y_copy, k, src, dst)
    for k, src, dst in (
        (0, own_sqx, sqx), (2, own_ssx, ssx), (3, own_nbx, nbx), (4, own_dqg, dqg),
        (5, own_sdx, sdx),
    ):
        wait_out(x_copy, k, src, dst)
    for j in (1, 3, 2):
        ps_copy((t + j) % NT).wait_send()
    for u in range(4):
        for j in (1, 3, 2):
            st_copy(u, j).wait_send()
    for stream in range(4):
        for step in range(RING[stream]):
            ring(stream, step).wait_send()
    for b in range(NZ):
        for half in range(2):
            partner(b, c, half).wait_send()
    most = pl.ds(0, (NS - 1) * 16)
    all_out(0, oute.at[most])
    all_out(1, outq.at[most, halves[0]])
    all_out(4, outq.at[most, halves[1]])
    all_out(2, rq.at[most])
    all_out(3, re.at[most])


def local(item_hidden, item_gain, send_item, pos_slot, hist_len, user_gain, query_weight):
    vmem = pltpu.VMEM
    dma = pltpu.SemaphoreType.DMA
    quarter = lambda kind: vmem((4, 256, 256), kind)
    grad, loss = pl.pallas_call(
        kernel,
        out_shape=(
            jax.ShapeDtypeStruct((64, 1024), F32),
            jax.ShapeDtypeStruct((4, 1, HIST), F32),
        ),
        in_specs=[pl.BlockSpec(memory_space=pltpu.SMEM)]
        + [pl.BlockSpec(memory_space=pltpu.VMEM)] * 6,
        out_specs=(
            pl.BlockSpec(memory_space=pltpu.VMEM),
            pl.BlockSpec(memory_space=pltpu.VMEM),
        ),
        scratch_shapes=[
            vmem((4, 64, 1024), BF16),
            vmem((4, 1, 1024), F32),
            vmem((8, 2, 64, 1024), BF16),
            vmem((4, 16, 256), F32),
            quarter(BF16),
            quarter(BF16),
            vmem((1024, 256), BF16),
            vmem((1024, 256), BF16),
            quarter(BF16),
            quarter(BF16),
            vmem((256, 1024), BF16),
            quarter(BF16),
            quarter(BF16),
            vmem((4, 8, 256), F32),
            vmem((256, HIST), F32),
            vmem((256, 256), F32),
            vmem((256, HIST), F32),
            vmem((256, HIST), F32),
            vmem((4, 2 * HIST), jnp.int32),
            vmem((256, 1024), BF16),
            vmem((1024, 256), BF16),
            vmem((512, HIST), F32),
            vmem((4, 1, HIST), F32),
            vmem((4, 1024, 256), BF16),
            vmem((4, 512, 256), BF16),
            vmem((4, 512, 256), BF16),
            vmem((4, 512, 256), BF16),
            vmem((8, 512, HIST), BF16),
            vmem((4, 512, 256), F32),
            vmem((4, 4, HIST, HIST), BF16),
            vmem((4, 2, HIST, HIST), F32),
            vmem((4, HIST, HIST), BF16),
            vmem((512, HIST), F32),
            vmem((4, 1, HIST), F32),
            quarter(F32),
            quarter(F32),
            quarter(BF16),
            quarter(BF16),
            vmem((1024, 256), BF16),
            vmem((1024, 256), BF16),
            quarter(BF16),
            vmem((4, 64, 1024), BF16),
            vmem((4, 64, 1024), BF16),
            vmem((4, 64, 256), F32),
            vmem((4, 64, 256), F32),
            vmem((4, 8, 256), F32),
            vmem((4, 8, 256), F32),
            vmem((4, 8, 256), F32),
            dma((10, 4)),
            dma((10, 4)),
            dma((5, 4)),
            dma((5, 4)),
            dma((4, 4)),
            dma((4, 4)),
            dma((8, 2)),
            dma((8, 2)),
            dma((5,)),
            dma((5,)),
        ],
        compiler_params=pltpu.CompilerParams(
            collective_id=0, has_side_effects=True, vmem_limit_bytes=60 * 1024 * 1024
        ),
    )(
        hist_len, item_hidden, query_weight.T, item_gain, user_gain, send_item[0].T, pos_slot
    )
    return (grad, loss[:, 0, 0])


def solution(mesh):
    placed = (
        P("sect", "tp"),
        P("tp"),
        P("sect", None, None),
        P("sect", None),
        P("sect"),
        P("tp"),
        P("tp", "sect"),
    )
    return jax.shard_map(
        local, mesh=mesh, in_specs=placed, out_specs=(P("sect", "tp"), P("sect")), check_vma=False
    )
```

time: 138 us -> 115 us (0.83); the launches traced: 136 us -> 115 us
  Pallas kernels: 128 us -> 111 us
  local copies, waits for them, and re-layouts: 6.72 us -> 2.95 us
    pallas_call x1, Pallas kernels: 128 us -> 111 us  [local(): pl.pallas_call(kernel, out_shape=(jax.ShapeDtypeStruct((64, 1024), F32),...]
    unnamed x14 -> x3, local copies, waits for them, and re-layouts: 4.05 us -> 2.33 us
where the time goes in v2:
time: 115 us
  Pallas kernels  111 us (97%)
  local copies, waits for them, and re-layouts  2.95 us (3%)
    pallas_call x1, Pallas kernels, local(): pl.pallas_call(kernel, out_shape=(jax.ShapeDtypeStruct((64, 1024), F32),...  111 us
    unnamed x3, local copies, waits for them, and re-layouts  2.33 us

profile of v2, /device:TPU:1, one launch (start us, length us, event | category | flops | bytes accessed | tf_op | source)
XLA Modules:
  0.0 114.7 jit_solution(10052489542515816690)
XLA Ops:
  0.6 111.1 %shard_map.86 = (f32[64,1024]{1,0:T(8,128)}, f32[4,1,128]{2,1,0:T(1,128)}) custom-call(s32[4]{0:T(128)} %len_ref.1, bf16[64,1024]{1,0:T(8,128)(2,1)} %hidden_ref.1, bf16[64,1024]{1,0:T(8,128)(2,1)} %bitcast.4, bf16[1024]{0:T(1024)(128)(2,1)} %gi_ref.1, bf16[1024]{0:T(1024)(128)(2,1)} %gu_ref.1, s32[4,64]{1,0:T(4,128)} %bitcast.5, s32[4,192]{1,0:T(4,128)} %pos_ref.1), custom_call_target="tpu_custom_call" | custom-call | tf_op jit(solution)/shard_map/pallas_call | solution.py:643
  111.7 0.0 copy-start
  111.7 0.7 copy-done
  112.4 0.6 slice_reduce_fusion
  113.0 1.7 %copy.10 = f32[64,1024]{1,0:T(8,128)} copy(f32[64,1024]{1,0:T(8,128)} %get-tuple-element.8) | data formatting | bytes 524288
Async XLA Ops:
  111.7 0.7 copy-start

commit v3 on v2

--- a/solution.py
+++ b/solution.py
@@ -93,10 +93,11 @@
 def kernel(
     len_ref, hidden_ref, w_ref, gi_ref, gu_ref, send_ref, pos_ref,
     grad_ref, loss_ref,
-    hd, selb, wt, sqx, ps, pr, oute, outq, bufe, bufq, gt, nrm, knb, ssx, sqm, q32,
-    rcol, rscol, pos_s, hot, hott, sqf_s, sqc_s,
-    rc_s, kn_s, v_s, qn_s, w_s, o_s, st_r, dsc, dneg_s, gfol, grow,
-    av, ae, dqo, eo, rq, re, dqg, gws, gwr, es, er, nbx, sdx, sdy,
+    hd, selb, wt, sqx, ps, pr, oute, outq, bufe, bufq, gt, nrm, knb, sqo, sqi, sqm, rsm, q32,
+    rcol, rscol, pos_s, hot, hott, sqf_s, sqc_s, gain_s,
+    rc_s, kn_s, v_s, qn_s, w_s, o_s, st_r, dsc, dneg_s, dnegt_s, gfol, grow,
+    dout_t, dq_t, dk_s, dv_s, drc_s, nbs, dqo, eo, rq, re, sco, sci,
+    dqg, gws, gwr, es, er, sdx, sdy,
     xs, xr, ys, yr, ring_s, ring_r, par_s, par_r, a2a_s, a2a_r,
 ):
     me = lax.axis_index("sect")
@@ -181,6 +182,18 @@
 
         def step(j, carry):
             copy(j).start()
+            return carry
+
+        lax.fori_loop(1, 16, step, 0)
+
+    def to_matched(k, src_of, dst):
+        pltpu.make_async_copy(src_of(blk), dst.at[blk], a2a_r.at[k]).start()
+
+        def step(j, carry):
+            b = (blk + j) % 16
+            send(
+                src_of(b), dst.at[blk], a2a_s.at[k], a2a_r.at[k], sect_of(b // 2, y, b % 2), t
+            ).start()
             return carry
 
         lax.fori_loop(1, 16, step, 0)
@@ -276,6 +289,7 @@
             hott[first : first + HIST, :] = jnp.transpose(picked).astype(BF16)
 
     advance(0)
+    advance(1)
     wait_in(y_from, 0, own_hd, hd)
     gi = gi_ref[...].astype(F32).reshape(1, 1024)
     gu = gu_ref[...].astype(F32).reshape(1, 1024)
@@ -308,25 +322,32 @@
 
     partners_in(0)
     project(0)
+    partners_in(1)
+    project(1)
+    advance(2)
     hidden = hd[...].reshape(256, 1024).astype(F32)
     sqx[t, pl.ds(0, 8), :] = row_sums(hidden * hidden)
     gained = hidden * gi
     sqx[t, pl.ds(8, 8), :] = row_sums(gained * gained)
     own_sqx = lambda peer: sqx.at[t]
     start3(x_copy, 0, own_sqx, sqx)
-    advance(1)
-    partners_in(1)
-    project(1)
+    partners_in(2)
+    project(2)
     wait_in(y_from, 1, own_sel, selb)
     picks = jnp.maximum(jnp.maximum(selb[0], selb[1]), jnp.maximum(selb[2], selb[3]))
     gt[...] = one_hot(picks.astype(jnp.int32), 256).astype(BF16)
-    advance(2)
-    partners_in(2)
-    project(2)
+    for q in range(4):
+        gain_s[q] = jnp.concatenate(
+            [gu[:, q * HD : (q + 1) * HD], gu[:, (4 + q) * HD : (5 + q) * HD]], axis=1
+        )
     wait_in(x_from, 0, own_sqx, sqx)
     sums = sqx[0] + sqx[1] + sqx[2] + sqx[3]
     r_row = lax.rsqrt(sums[0:1] * (1.0 / D) + EPS)
-    rs_row = lax.rsqrt(r_row * r_row * sums[8:9] * (1.0 / D) + EPS)
+    sq_item = r_row * r_row * sums[8:9]
+    rs_row = lax.rsqrt(sq_item * (1.0 / D) + EPS)
+    sq_out = jnp.sum(mm(row_parts(sq_item), gt[...], 1, 0), axis=0, keepdims=True)
+    for b in range(NZ):
+        sqo[b] = sq_out[:, b * HD : (b + 1) * HD]
     rcol[...] = columns(r_row)
     rscol[...] = columns(rs_row)
     pieces = []
@@ -343,6 +364,7 @@
     partners_in(3)
     project(3)
     both = slice(0, 256)
+    to_matched(5, lambda b: sqo.at[b // 2], sqi)
     to_readers(0, oute, bufe, both)
     pr[t] = ps[t]
     for j in (1, 3, 2):
@@ -360,40 +382,33 @@
     to_readers(1, outq, bufq, halves[0])
     to_readers(4, outq, bufq, halves[1])
 
+    off = (me % 8) * 16
+    blocks = jnp.where((iota((256, 16), 0) >> 4) == iota((256, 16), 1), 1.0, 0.0).astype(BF16)
+    in_lane = iota((256, HD), 1) == off + (iota((256, HD), 0) & 15)
+    all_in(5, sqi)
+    came = jnp.concatenate([sqi[b] for b in range(16)], axis=0)
+    high, mid, low = split3(came)
+    wide = mm(blocks, high, 1, 0) + mm(blocks, mid, 1, 0) + mm(blocks, low, 1, 0)
+    sqm[...] = jnp.broadcast_to(lane_sum(jnp.where(in_lane, wide, 0.0)), (256, HD))
+    rsm[...] = lax.rsqrt(sqm[...] * (1.0 / D) + EPS)
+    sqf_s[...] = jnp.broadcast_to(
+        lane_sum(mm(hott[0:512], lane_parts(sqm[...]), 1, 0)), (512, HIST)
+    )
+    sqc = jnp.sum(mm(lane_parts(sqm[...]), hot[:, 512:1024], 0, 0), axis=0, keepdims=True)
+    for u in range(4):
+        sqc_s[u] = sqc[:, u * HIST : (u + 1) * HIST]
+    twice = lambda values: jnp.concatenate([values, values], axis=1)
     all_in(0, bufe)
-    part = jnp.zeros((8, 256), F32)
     for q in range(4):
-        rows = bufe[q].astype(F32)
-        part = part + row_sums(rows * rows)
-    ssx[t] = part
-    own_ssx = lambda peer: ssx.at[t]
-    start3(x_copy, 2, own_ssx, ssx)
-    for q in range(4):
-        rc_s[q] = mm(hott[...], bufe[q], 1, 0).astype(BF16)
-
-    def gain_of(q):
-        return jnp.concatenate(
-            [gu[:, q * HD : (q + 1) * HD], gu[:, (4 + q) * HD : (5 + q) * HD]], axis=1
-        )
-
-    wait_in(x_from, 2, own_ssx, ssx)
-    sq_row = (ssx[0] + ssx[1] + ssx[2] + ssx[3])[0:1]
-    sqm[...] = columns(sq_row)
-    rs = lax.rsqrt(sqm[...] * (1.0 / D) + EPS)[:, 0:1]
-    for q in range(4):
-        low = (bufe[q].astype(F32) * rs * gain_of(q)).astype(BF16)
+        low = (bufe[q].astype(F32) * twice(rsm[...]) * gain_s[q]).astype(BF16)
         nrm[q] = low
         heads, _ = norm_heads(low.astype(F32))
         knb[q] = jnp.concatenate(heads, axis=1).astype(BF16)
     for q in range(4):
         kn_s[q] = mm(hott[0:512], knb[q], 1, 0).astype(BF16)
         v_s[q] = mm(hott[0:512], nrm[q], 1, 0).astype(BF16)
-    sqf_s[...] = jnp.broadcast_to(
-        lane_sum(mm(hott[0:512], lane_parts(sqm[...]), 1, 0)), (512, HIST)
-    )
-    sqc = jnp.sum(mm(row_parts(sq_row), hot[:, 512:1024], 1, 0), axis=0, keepdims=True)
-    for u in range(4):
-        sqc_s[u] = sqc[:, u * HIST : (u + 1) * HIST]
+    for q in range(4):
+        rc_s[q] = mm(hott[...], bufe[q], 1, 0).astype(BF16)
 
     scale = HD ** (-0.5)
     row_id = iota((HIST, HIST), 0)
@@ -458,7 +473,7 @@
         all_in(1 if par == 0 else 4, outq.at[:, halves[0]])
         for q in range(4):
             qn_s[q, :, halves[par]] = mm(hott[0:512], bufq[q, :, halves[par]], 1, 0).astype(BF16)
-        lax.fori_loop(0, 4, step, 0)
+        lax.fori_loop(0, 4, step, 0, unroll=2)
 
     def losses(u, carry):
         for j in (1, 3, 2):
@@ -492,7 +507,9 @@
             -rn * rn * (dtl * tl + lane_sum(dnl * nl)), (HIST, HIST)
         )
         dsc[u, 1] = jnp.broadcast_to(dtl * (SOFT * rn * rf), (HIST, HIST))
-        dneg_s[u] = (dnl * (SOFT * rn * rc)).astype(BF16)
+        dneg = dnl * (SOFT * rn * rc)
+        dneg_s[u] = dneg.astype(BF16)
+        dnegt_s[u] = jnp.transpose(dneg).astype(BF16)
         dsqf = jnp.broadcast_to(-0.5 * dtl * tl * rf * rf, (HIST, HIST))
         gfol[user_rows(u)] = pltpu.roll(dsqf, 1, 0)
         grow[u] = -0.5 * rc * rc * jnp.sum(dnl * nl, axis=0, keepdims=True)
@@ -505,74 +522,77 @@
         for u in range(4):
             span = slice(u * HIST, (u + 1) * HIST)
             cspan = slice((4 + u) * HIST, (5 + u) * HIST)
-            twice_down = jnp.concatenate([dsc[u, 0]] * 2, axis=1)
-            dhit = jnp.concatenate([dsc[u, 1]] * 2, axis=1)
+            dhit = twice(dsc[u, 1])
             out = o_s[q, span]
             rows = rc_s[q, span].astype(F32)
-            cands = rc_s[q, cspan]
-            dneg = dneg_s[u]
-            dout = twice_down * out + dhit * follow_of(rows) + mm(dneg, cands, 1, 0)
-            rc_s[q, cspan] = mm(dneg, out.astype(BF16), 0, 0).astype(BF16)
-            rc_s[q, span] = (dout + pltpu.roll(dhit * out, 1, 0)).astype(BF16)
-            dout_low = dout.astype(BF16)
+            dout = (
+                twice(dsc[u, 0]) * out
+                + dhit * follow_of(rows)
+                + mm(dneg_s[u], rc_s[q, cspan], 1, 0)
+            )
+            dout_t[span] = dout.astype(BF16)
+            drc_s[q, span] = (dout + pltpu.roll(dhit * out, 1, 0)).astype(BF16)
+            drc_s[q, cspan] = mm(dnegt_s[u], out.astype(BF16), 1, 0).astype(BF16)
+        for u in range(4):
+            span = slice(u * HIST, (u + 1) * HIST)
             for par in range(2):
                 lanes = halves[par]
-                qn = qn_s[q, span, lanes]
-                kn = kn_s[q, span, lanes]
-                grad = dout_low[:, lanes]
+                grad = dout_t[span, lanes]
                 weights = w_s[2 * q + par, span]
                 wide = weights.astype(F32)
                 dw = mm(grad, v_s[q, span, lanes], 1, 1)
                 ds = (wide * (dw - lane_sum(dw * wide)) * scale).astype(BF16)
-                qn_s[q, span, lanes] = mm(ds, kn, 1, 0).astype(BF16)
-                kn_s[q, span, lanes] = mm(ds, qn, 0, 0).astype(BF16)
-                v_s[q, span, lanes] = mm(weights, grad, 0, 0).astype(BF16)
-        dqo[q] = mm(hot[:, 0:512], qn_s[q], 1, 0).astype(BF16)
+                dq_t[span, lanes] = mm(ds, kn_s[q, span, lanes], 1, 0).astype(BF16)
+                dk_s[q, span, lanes] = mm(ds, qn_s[q, span, lanes], 0, 0).astype(BF16)
+                dv_s[q, span, lanes] = mm(weights, grad, 0, 0).astype(BF16)
+        dqo[q] = mm(hot[:, 0:512], dq_t[...], 1, 0).astype(BF16)
         to_group(2, dqo, rq, q, i == 3)
         return carry
 
     lax.fori_loop(0, 4, backward_quarter, 0)
 
-    rs = lax.rsqrt(sqm[...] * (1.0 / D) + EPS)[:, 0:1]
-    part = jnp.zeros((8, 256), F32)
-    for q in range(4):
-        dk = mm(hot[:, 0:512], kn_s[q], 1, 0)
-        dn = mm(hot[:, 0:512], v_s[q], 1, 0) + norm_heads_back(nrm[q].astype(F32), dk)
-        dn = dn * gain_of(q)
-        part = part + row_sums(dn * bufe[q].astype(F32))
-        av[q] = dn
-    nbx[t] = part
-    own_nbx = lambda peer: nbx.at[t]
-    start3(x_copy, 3, own_nbx, nbx)
+    nbs[...] = jnp.zeros(nbs.shape, F32)
+
+    def return_quarter(i, carry):
+        q = (y + 1 + i) % 4
+        dk = mm(hot[:, 0:512], dk_s[q], 1, 0)
+        dn = mm(hot[:, 0:512], dv_s[q], 1, 0) + norm_heads_back(nrm[q].astype(F32), dk)
+        dn = dn * gain_s[q]
+        nbs[...] += jnp.broadcast_to(lane_sum(dn * bufe[q].astype(F32)), (256, HD))
+        eo[q] = (mm(hot[...], drc_s[q], 1, 0) + dn * twice(rsm[...])).astype(BF16)
+        to_group(3, eo, re, q, i == 3)
+        return carry
+
+    lax.fori_loop(0, 4, return_quarter, 0)
     gsq = lane_sum(mm(hot[:, 0:512], lane_parts(gfol[...]), 1, 0)) + lane_sum(
         mm(
             hot[:, 512:1024],
             row_parts(jnp.concatenate([grow[u] for u in range(4)], axis=1)), 1, 1,
         )
     )
-    for q in range(4):
-        ae[q] = mm(hot[...], rc_s[q], 1, 0) + av[q] * rs
-    wait_in(x_from, 3, own_nbx, nbx)
-    nb = columns((nbx[0] + nbx[1] + nbx[2] + nbx[3])[0:1])[:, 0:1]
-    slot_term = 2.0 * (gsq - (0.5 / D) * rs * rs * rs * nb)
-    for q in range(4):
-        eo[q] = (ae[q] + bufe[q].astype(F32) * slot_term).astype(BF16)
+    placed = []
+    for values in (jnp.broadcast_to(gsq, (256, HD)), nbs[...]):
+        high, mid, low = split3(jnp.where(in_lane, values, 0.0))
+        placed.append(mm(blocks, high, 0, 0) + mm(blocks, mid, 0, 0) + mm(blocks, low, 0, 0))
+    for b in range(16):
+        sco[b] = jnp.concatenate([part[b : b + 1] for part in placed], axis=1)
+    to_matched(6, lambda b: sco.at[b], sci)
 
     all_in(2, rq)
     dq_item = norm_heads_back(q32[...], mm(gt[...], rq[...], 1, 0)).astype(BF16)
     dqg[t] = dq_item
     own_dqg = lambda peer: dqg.at[t]
     start3(x_copy, 4, own_dqg, dqg)
-    sdx[t] = row_sums(dq_item.astype(F32) * q32[...])
+    all_in(6, sci)
+    pairs = [sci[2 * b] + sci[2 * b + 1] for b in range(NZ)]
+    item_terms = []
+    for lanes in (slice(0, HD), slice(HD, 2 * HD)):
+        row = jnp.concatenate([pair[:, lanes] for pair in pairs], axis=1)
+        item_terms.append(jnp.sum(mm(row_parts(row), gt[...], 1, 1), axis=0, keepdims=True))
+    sdy[y, pl.ds(8, 8), :] = jnp.broadcast_to(item_terms[0], (8, 256))
+    sdx[t] = row_sums(dq_item.astype(F32) * q32[...]) + rs_row * item_terms[1]
     own_sdx = lambda peer: sdx.at[t]
     start3(x_copy, 5, own_sdx, sdx)
-
-    def return_group(i, carry):
-        group = (y + 1 + i) % 4
-        to_group(3, eo, re, group, i == 3)
-        return carry
-
-    lax.fori_loop(0, 4, return_group, 0)
     wait_in(x_from, 4, own_dqg, dqg)
     gws_of = lambda peer: gws.at[peer]
     acc = jnp.zeros((256, 1024), F32)
@@ -582,11 +602,11 @@
     start3(y_copy, 2, gws_of, gwr)
     gwr[y] = gws[y]
     wait_in(x_from, 5, own_sdx, sdx)
-    sdy[y] = sdx[0] + sdx[1] + sdx[2] + sdx[3]
+    sdy[y, pl.ds(0, 8), :] = sdx[0] + sdx[1] + sdx[2] + sdx[3]
     own_sdy = lambda peer: sdy.at[y]
     start3(y_copy, 4, own_sdy, sdy)
     all_in(3, re)
-    es[...] = mm(gt[...], re[...], 1, 0).reshape(4, 64, 256)
+    es[...] = mm(gt[...], re[...], 1, 0).astype(BF16).reshape(4, 64, 256)
     es_of = lambda peer: es.at[peer]
     start3(y_copy, 3, es_of, er)
     er[y] = es[y]
@@ -595,8 +615,9 @@
     emb = (hidden_ref[...].astype(F32) * rcol[mine, 0:1] * gi).astype(BF16).astype(F32)
     rs_own = rscol[mine, 0:1]
     wait_in(y_from, 4, own_sdy, sdy)
-    sqm[...] = columns((sdy[0] + sdy[1] + sdy[2] + sdy[3])[0:1])
-    coef = (-1.0 / D) * rs_own * rs_own * sqm[mine, 0:1]
+    last = sdy[0] + sdy[1] + sdy[2] + sdy[3]
+    sqm[...] = columns(2.0 * last[8:9] - (1.0 / D) * rs_row * rs_row * last[0:1])
+    coef = sqm[mine, 0:1]
     direct = emb * coef
     wait_in(y_from, 2, gws_of, gwr)
     gw = (
@@ -606,15 +627,14 @@
     for h in range(8):
         lanes = slice(h * HD, (h + 1) * HD)
         par, q = h // 4, h % 4
-        grad_ref[:, lanes] = er[q][:, par * HD : (par + 1) * HD] + gw[:, lanes]
+        grad_ref[:, lanes] = er[q, :, halves[par]].astype(F32) + gw[:, lanes]
 
     for k, src, dst in (
         (0, own_hd, hd), (1, own_sel, selb), (2, gws_of, gwr), (3, es_of, er), (4, own_sdy, sdy)
     ):
         wait_out(y_copy, k, src, dst)
     for k, src, dst in (
-        (0, own_sqx, sqx), (2, own_ssx, ssx), (3, own_nbx, nbx), (4, own_dqg, dqg),
-        (5, own_sdx, sdx),
+        (0, own_sqx, sqx), (4, own_dqg, dqg), (5, own_sdx, sdx)
     ):
         wait_out(x_copy, k, src, dst)
     for j in (1, 3, 2):
@@ -634,6 +654,8 @@
     all_out(4, outq.at[most, halves[1]])
     all_out(2, rq.at[most])
     all_out(3, re.at[most])
+    all_out(5, sqi.at[pl.ds(0, 15)])
+    all_out(6, sci.at[pl.ds(0, 15)])
 
 
 def local(item_hidden, item_gain, send_item, pos_slot, hist_len, user_gain, query_weight):
@@ -666,7 +688,9 @@
             vmem((256, 1024), BF16),
             quarter(BF16),
             quarter(BF16),
-            vmem((4, 8, 256), F32),
+            vmem((8, 1, HIST), F32),
+            vmem((16, 1, HIST), F32),
+            vmem((256, HIST), F32),
             vmem((256, HIST), F32),
             vmem((256, 256), F32),
             vmem((256, HIST), F32),
@@ -676,6 +700,7 @@
             vmem((1024, 256), BF16),
             vmem((512, HIST), F32),
             vmem((4, 1, HIST), F32),
+            vmem((4, 1, 256), F32),
             vmem((4, 1024, 256), BF16),
             vmem((4, 512, 256), BF16),
             vmem((4, 512, 256), BF16),
@@ -685,22 +710,28 @@
             vmem((4, 4, HIST, HIST), BF16),
             vmem((4, 2, HIST, HIST), F32),
             vmem((4, HIST, HIST), BF16),
+            vmem((4, HIST, HIST), BF16),
             vmem((512, HIST), F32),
             vmem((4, 1, HIST), F32),
-            quarter(F32),
-            quarter(F32),
+            vmem((512, 256), BF16),
+            vmem((512, 256), BF16),
+            vmem((4, 512, 256), BF16),
+            vmem((4, 512, 256), BF16),
+            vmem((4, 1024, 256), BF16),
+            vmem((256, HIST), F32),
             quarter(BF16),
             quarter(BF16),
             vmem((1024, 256), BF16),
             vmem((1024, 256), BF16),
+            vmem((16, 1, 256), F32),
+            vmem((16, 1, 256), F32),
             quarter(BF16),
             vmem((4, 64, 1024), BF16),
             vmem((4, 64, 1024), BF16),
-            vmem((4, 64, 256), F32),
-            vmem((4, 64, 256), F32),
+            vmem((4, 64, 256), BF16),
+            vmem((4, 64, 256), BF16),
             vmem((4, 8, 256), F32),
-            vmem((4, 8, 256), F32),
-            vmem((4, 8, 256), F32),
+            vmem((4, 16, 256), F32),
             dma((10, 4)),
             dma((10, 4)),
             dma((5, 4)),
@@ -709,8 +740,8 @@
             dma((4, 4)),
             dma((8, 2)),
             dma((8, 2)),
-            dma((5,)),
-            dma((5,)),
+            dma((7,)),
+            dma((7,)),
         ],
         compiler_params=pltpu.CompilerParams(
             collective_id=0, has_side_effects=True, vmem_limit_bytes=60 * 1024 * 1024

time: 115 us -> 119 us (1.035)
  Pallas kernels: 111 us -> 116 us
    pallas_call x1, Pallas kernels: 111 us -> 116 us  [local(): pl.pallas_call(kernel, out_shape=(jax.ShapeDtypeStruct((64, 1024), F32),...]
where the time goes in v3:
time: 119 us
  Pallas kernels  116 us (97%)
  local copies, waits for them, and re-layouts  2.95 us (2%)
    pallas_call x1, Pallas kernels, local(): pl.pallas_call(kernel, out_shape=(jax.ShapeDtypeStruct((64, 1024), F32),...  116 us

profile of v3, /device:TPU:1, one launch (start us, length us, event | category | flops | bytes accessed | tf_op | source)
XLA Modules:
  0.0 119.3 jit_solution(17105888152109154159)
XLA Ops:
  0.6 115.7 %shard_map.86 = (f32[64,1024]{1,0:T(8,128)}, f32[4,1,128]{2,1,0:T(1,128)}) custom-call(s32[4]{0:T(128)} %len_ref.1, bf16[64,1024]{1,0:T(8,128)(2,1)} %hidden_ref.1, bf16[64,1024]{1,0:T(8,128)(2,1)} %bitcast.4, bf16[1024]{0:T(1024)(128)(2,1)} %gi_ref.1, bf16[1024]{0:T(1024)(128)(2,1)} %gu_ref.1, s32[4,64]{1,0:T(4,128)} %bitcast.5, s32[4,192]{1,0:T(4,128)} %pos_ref.1), custom_call_target="tpu_custom_call" | custom-call | tf_op jit(solution)/shard_map/pallas_call | solution.py:665
  116.4 0.0 copy-start
  116.4 0.7 copy-done
  117.0 0.6 slice_reduce_fusion
  117.7 1.7 %copy.10 = f32[64,1024]{1,0:T(8,128)} copy(f32[64,1024]{1,0:T(8,128)} %get-tuple-element.8) | data formatting | bytes 524288
Async XLA Ops:
  116.4 0.7 copy-start

commit v4 on v3

--- a/solution.py
+++ b/solution.py
@@ -93,12 +93,12 @@
 def kernel(
     len_ref, hidden_ref, w_ref, gi_ref, gu_ref, send_ref, pos_ref,
     grad_ref, loss_ref,
-    hd, selb, wt, sqx, ps, pr, oute, outq, bufe, bufq, gt, nrm, knb, sqo, sqi, sqm, rsm, q32,
+    hd, selb, wt, sqx, sqy, ps, pr, oute, outq, bufe, bufq, gt, nrm, knb, sqo, sqi, sqm, rsm, q32,
     rcol, rscol, pos_s, hot, hott, sqf_s, sqc_s, gain_s,
-    rc_s, kn_s, v_s, qn_s, w_s, o_s, st_r, dsc, dneg_s, dnegt_s, gfol, grow,
+    rc_s, kn_s, v_s, qn_s, w_s, wt_s, p_t, ds_t, o_s, st_r, dsc, dneg_s, dnegt_s, gfol, grow,
     dout_t, dq_t, dk_s, dv_s, drc_s, nbs, dqo, eo, rq, re, sco, sci,
     dqg, gws, gwr, es, er, sdx, sdy,
-    xs, xr, ys, yr, ring_s, ring_r, par_s, par_r, a2a_s, a2a_r,
+    xs, xr, ys, yr, ring_s, ring_r, par_s, par_r, a2a_s, a2a_r, hello,
 ):
     me = lax.axis_index("sect")
     t = lax.axis_index("tp")
@@ -254,6 +254,7 @@
         pl.semaphore_signal(barrier, inc=1, device_id=(me, (t + j) % NT), device_id_type=MESH)
 
     hd[y] = hidden_ref[...]
+    sqx[t] = jnp.zeros((16, HIST), F32)
     wt[z, c] = w_ref[...]
     spread = jnp.where((iota((64, 1024), 1) >> 4) == iota((64, 1024), 0), 1.0, 0.0).astype(BF16)
     named = mm(send_ref[...].astype(F32).astype(BF16), spread, 1, 0)
@@ -265,6 +266,22 @@
     selb[y] = jnp.where((((lane >> 2) & 3) == y) & (pick >= 0.0), pick + base, -1.0)
     pl.semaphore_wait(barrier, 7 + 2 + NT - 1)
 
+    def greet(step):
+        for way in range(2):
+            if step < 4 - way:
+                peer = (z + 1) % NZ if way == 0 else (z + NZ - 1) % NZ
+                pl.semaphore_signal(
+                    hello.at[way, step], inc=1, device_id=(sect_of(peer, y, c), t),
+                    device_id_type=MESH,
+                )
+
+    def relay(step):
+        for way in range(2):
+            if step < 4 - way:
+                pl.semaphore_wait(hello.at[way, step], 1)
+        greet(step + 1)
+
+    greet(0)
     own_hd = lambda peer: hd.at[y]
     own_sel = lambda peer: selb.at[y]
     for stream in (0, 2, 1, 3):
@@ -273,6 +290,15 @@
     start3(y_copy, 1, own_sel, selb)
     for half in range(2):
         partner(z, c, half).start()
+
+    gi = gi_ref[...].astype(F32).reshape(1, 1024)
+    gu = gu_ref[...].astype(F32).reshape(1, 1024)
+    hidden = hidden_ref[...].astype(F32)
+    gained = hidden * gi
+    sqx[t, pl.ds(0, 8), 0:64] = row_sums(hidden * hidden)
+    sqx[t, pl.ds(8, 8), 0:64] = row_sums(gained * gained)
+    own_sqx = lambda peer: sqx.at[t]
+    start3(x_copy, 0, own_sqx, sqx)
 
     slots = pos_ref[...]
     owner = slots >> 2
@@ -289,10 +315,19 @@
             hott[first : first + HIST, :] = jnp.transpose(picked).astype(BF16)
 
     advance(0)
+    relay(0)
+    wait_in(x_from, 0, own_sqx, sqx)
+    sums = sqx[0] + sqx[1] + sqx[2] + sqx[3]
+    r_row = lax.rsqrt(sums[0:1] * (1.0 / D) + EPS)
+    sq_item = r_row * r_row * sums[8:9]
+    rs_row = lax.rsqrt(sq_item * (1.0 / D) + EPS)
+    sqy[y] = jnp.concatenate([r_row, rs_row, sq_item] + [r_row] * 5, axis=0)
+    own_sqy = lambda peer: sqy.at[y]
+    start3(y_copy, 5, own_sqy, sqy)
+    relay(1)
     advance(1)
+    relay(2)
     wait_in(y_from, 0, own_hd, hd)
-    gi = gi_ref[...].astype(F32).reshape(1, 1024)
-    gu = gu_ref[...].astype(F32).reshape(1, 1024)
     lhs = (hd[...].reshape(256, 1024).astype(F32) * (gi * gu)).astype(BF16)
 
     near = z // 2
@@ -322,34 +357,20 @@
 
     partners_in(0)
     project(0)
-    partners_in(1)
-    project(1)
-    advance(2)
-    hidden = hd[...].reshape(256, 1024).astype(F32)
-    sqx[t, pl.ds(0, 8), :] = row_sums(hidden * hidden)
-    gained = hidden * gi
-    sqx[t, pl.ds(8, 8), :] = row_sums(gained * gained)
-    own_sqx = lambda peer: sqx.at[t]
-    start3(x_copy, 0, own_sqx, sqx)
-    partners_in(2)
-    project(2)
     wait_in(y_from, 1, own_sel, selb)
     picks = jnp.maximum(jnp.maximum(selb[0], selb[1]), jnp.maximum(selb[2], selb[3]))
     gt[...] = one_hot(picks.astype(jnp.int32), 256).astype(BF16)
-    for q in range(4):
-        gain_s[q] = jnp.concatenate(
-            [gu[:, q * HD : (q + 1) * HD], gu[:, (4 + q) * HD : (5 + q) * HD]], axis=1
-        )
-    wait_in(x_from, 0, own_sqx, sqx)
-    sums = sqx[0] + sqx[1] + sqx[2] + sqx[3]
-    r_row = lax.rsqrt(sums[0:1] * (1.0 / D) + EPS)
-    sq_item = r_row * r_row * sums[8:9]
-    rs_row = lax.rsqrt(sq_item * (1.0 / D) + EPS)
-    sq_out = jnp.sum(mm(row_parts(sq_item), gt[...], 1, 0), axis=0, keepdims=True)
+    wait_in(y_from, 5, own_sqy, sqy)
+    rcol[...] = jnp.concatenate([columns(sqy[b, 0:1])[0:64] for b in range(4)], axis=0)
+    rscol[...] = jnp.concatenate([columns(sqy[b, 1:2])[0:64] for b in range(4)], axis=0)
+    sq_out = jnp.zeros((8, 1024), F32)
+    for b in range(4):
+        sq_out = sq_out + mm(
+            row_parts(sqy[b, 2:3])[:, 0:64], gt[b * 64 : (b + 1) * 64, :], 1, 0
+        )
+    sq_out = jnp.sum(sq_out, axis=0, keepdims=True)
     for b in range(NZ):
         sqo[b] = sq_out[:, b * HD : (b + 1) * HD]
-    rcol[...] = columns(r_row)
-    rscol[...] = columns(rs_row)
     pieces = []
     for par in range(2):
         head = par * 4 + y
@@ -360,12 +381,22 @@
             gain = gain + jnp.where(head == h, gi[:, h * HD : (h + 1) * HD], 0.0)
         pieces.append((piece * rcol[...] * gain).astype(BF16))
     oute[...] = mm(gt[...], jnp.concatenate(pieces, axis=1), 0, 0).astype(BF16)
+    partners_in(1)
+    project(1)
+    advance(2)
+    relay(3)
+    both = slice(0, 256)
+    to_matched(5, lambda b: sqo.at[b // 2], sqi)
+    to_readers(0, oute, bufe, both)
+    partners_in(2)
+    project(2)
     advance(3)
     partners_in(3)
     project(3)
-    both = slice(0, 256)
-    to_matched(5, lambda b: sqo.at[b // 2], sqi)
-    to_readers(0, oute, bufe, both)
+    for q in range(4):
+        gain_s[q] = jnp.concatenate(
+            [gu[:, q * HD : (q + 1) * HD], gu[:, (4 + q) * HD : (5 + q) * HD]], axis=1
+        )
     pr[t] = ps[t]
     for j in (1, 3, 2):
         sender = (t + j) % NT
@@ -432,24 +463,27 @@
     def user_rows(u):
         return pl.ds(pl.multiple_of(u * HIST, HIST), HIST)
 
-    def attend(u, par):
-        span = user_rows(u)
+    def attend(first, par):
         lanes = halves[par]
-        mask = jnp.where((col_id <= row_id) & (col_id < len_ref[u]), 1.0, 0.0)
-        for q in range(4):
-            weights = jnp.exp(mm(qn_s[q, span, lanes], kn_s[q, span, lanes], 1, 1) * scale) * mask
-            weights = (weights * (1.0 / lane_sum(weights))).astype(BF16)
-            w_s[2 * q + par, span] = weights
+        tasks = [(first + k, q, 4 * k + q) for k in range(2) for q in range(4)]
+        for u, q, slot in tasks:
+            span = user_rows(u)
+            p_t[slot] = mm(qn_s[q, span, lanes], kn_s[q, span, lanes], 1, 1)
+        for u, q, slot in tasks:
+            mask = (col_id <= row_id) & (col_id < len_ref[u])
+            weights = jnp.where(mask, jnp.exp(p_t[slot] * scale), 0.0)
+            w_s[2 * q + par, user_rows(u)] = (weights * (1.0 / lane_sum(weights))).astype(BF16)
+        for u, q, slot in tasks:
+            span = user_rows(u)
             o_s[q, span, lanes] = rc_s[q, span, lanes].astype(F32) + mm(
-                weights, v_s[q, span, lanes], 1, 0
+                w_s[2 * q + par, span], v_s[q, span, lanes], 1, 0
             )
 
-    def first_half(u, carry):
-        attend(u, 0)
+    def first_half(i, carry):
+        attend(2 * i, 0)
         return carry
 
-    def second_half(u, carry):
-        attend(u, 1)
+    def score(u):
         span = user_rows(u)
         cspan = user_rows(u + 4)
         own = jnp.zeros((HIST, 1), F32)
@@ -467,13 +501,25 @@
         st_r[t, u] = stats.astype(BF16)
         for j in (2, 1, 3):
             st_copy(u, j).start()
+
+    def second_half(i, carry):
+        attend(2 * i, 1)
+        score(2 * i)
+        score(2 * i + 1)
+        return carry
+
+    def turn_weights(k, carry):
+        for u in range(4):
+            span = slice(u * HIST, (u + 1) * HIST)
+            wt_s[k, span] = jnp.transpose(w_s[k, span].astype(F32)).astype(BF16)
         return carry
 
     for par, step in ((0, first_half), (1, second_half)):
         all_in(1 if par == 0 else 4, outq.at[:, halves[0]])
         for q in range(4):
             qn_s[q, :, halves[par]] = mm(hott[0:512], bufq[q, :, halves[par]], 1, 0).astype(BF16)
-        lax.fori_loop(0, 4, step, 0, unroll=2)
+        lax.fori_loop(0, 2, step, 0)
+    lax.fori_loop(0, 8, turn_weights, 0)
 
     def losses(u, carry):
         for j in (1, 3, 2):
@@ -533,18 +579,23 @@
             dout_t[span] = dout.astype(BF16)
             drc_s[q, span] = (dout + pltpu.roll(dhit * out, 1, 0)).astype(BF16)
             drc_s[q, cspan] = mm(dnegt_s[u], out.astype(BF16), 1, 0).astype(BF16)
-        for u in range(4):
-            span = slice(u * HIST, (u + 1) * HIST)
-            for par in range(2):
-                lanes = halves[par]
-                grad = dout_t[span, lanes]
-                weights = w_s[2 * q + par, span]
-                wide = weights.astype(F32)
-                dw = mm(grad, v_s[q, span, lanes], 1, 1)
-                ds = (wide * (dw - lane_sum(dw * wide)) * scale).astype(BF16)
-                dq_t[span, lanes] = mm(ds, kn_s[q, span, lanes], 1, 0).astype(BF16)
-                dk_s[q, span, lanes] = mm(ds, qn_s[q, span, lanes], 0, 0).astype(BF16)
-                dv_s[q, span, lanes] = mm(weights, grad, 0, 0).astype(BF16)
+        tasks = [
+            (slice(u * HIST, (u + 1) * HIST), halves[par], par, 2 * u + par)
+            for u in range(4)
+            for par in range(2)
+        ]
+        for span, lanes, par, slot in tasks:
+            p_t[slot] = mm(dout_t[span, lanes], v_s[q, span, lanes], 1, 1)
+        for span, lanes, par, slot in tasks:
+            dw = p_t[slot]
+            wide = w_s[2 * q + par, span].astype(F32)
+            ds_t[slot] = (wide * (dw - lane_sum(dw * wide)) * scale).astype(BF16)
+        for span, lanes, par, slot in tasks:
+            dq_t[span, lanes] = mm(ds_t[slot], kn_s[q, span, lanes], 1, 0).astype(BF16)
+            dk_s[q, span, lanes] = mm(ds_t[slot], qn_s[q, span, lanes], 0, 0).astype(BF16)
+            dv_s[q, span, lanes] = mm(wt_s[2 * q + par, span], dout_t[span, lanes], 1, 0).astype(
+                BF16
+            )
         dqo[q] = mm(hot[:, 0:512], dq_t[...], 1, 0).astype(BF16)
         to_group(2, dqo, rq, q, i == 3)
         return carry
@@ -560,7 +611,6 @@
         dn = dn * gain_s[q]
         nbs[...] += jnp.broadcast_to(lane_sum(dn * bufe[q].astype(F32)), (256, HD))
         eo[q] = (mm(hot[...], drc_s[q], 1, 0) + dn * twice(rsm[...])).astype(BF16)
-        to_group(3, eo, re, q, i == 3)
         return carry
 
     lax.fori_loop(0, 4, return_quarter, 0)
@@ -578,11 +628,59 @@
         sco[b] = jnp.concatenate([part[b : b + 1] for part in placed], axis=1)
     to_matched(6, lambda b: sco.at[b], sci)
 
+    def return_group(i, carry):
+        to_group(3, eo, re, (y + 1 + i) % 4, i == 3)
+        return carry
+
+    lax.fori_loop(0, 4, return_group, 0)
+
     all_in(2, rq)
     dq_item = norm_heads_back(q32[...], mm(gt[...], rq[...], 1, 0)).astype(BF16)
-    dqg[t] = dq_item
-    own_dqg = lambda peer: dqg.at[t]
-    start3(x_copy, 4, own_dqg, dqg)
+    dqg[t] = dq_item.reshape(4, 64, 256)
+    chunks = (((y + 2) % NY, (y + 1) % NY), ((y + 3) % NY, y))
+
+    def dq_copy(part, j):
+        peer = (t + j) % NT
+        return [
+            send(
+                dqg.at[t, b], dqg.at[t, b], xs.at[(2, 3, 4, 10)[2 * part + k], peer],
+                xr.at[(2, 3, 4, 10)[2 * part + k], t], me, peer,
+            )
+            for k, b in enumerate(chunks[part])
+        ]
+
+    def dq_from(part, j):
+        sender = (t + NT - j) % NT
+        return [
+            send(
+                dqg.at[t, b], dqg.at[sender, b], xs.at[(2, 3, 4, 10)[2 * part + k], sender],
+                xr.at[(2, 3, 4, 10)[2 * part + k], sender], me, sender,
+            )
+            for k, b in enumerate(chunks[part])
+        ]
+
+    for part in range(2):
+        for j in (2, 1, 3):
+            for copy in dq_copy(part, j):
+                copy.start()
+    dots = row_sums(dq_item.astype(F32) * q32[...])
+    gws_of = lambda peer: gws.at[peer]
+    for part in range(2):
+        for j in (1, 3, 2):
+            for copy in dq_from(part, j):
+                copy.wait_recv()
+        acc = jnp.zeros((128, 1024), F32)
+        for tt in range(NT):
+            acc = acc + mm(
+                jnp.concatenate([dqg[tt, b] for b in chunks[part]], axis=0),
+                wt[2 * tt : 2 * tt + 2].reshape(256, 1024), 1, 0,
+            )
+        acc = acc.astype(BF16)
+        for k, b in enumerate(chunks[part]):
+            gws[b] = acc[k * 64 : (k + 1) * 64]
+        for j in ((2, 1), (3,))[part]:
+            y_copy(2, gws_of, gwr, j).start()
+    gwr[y] = gws[y]
     all_in(6, sci)
     pairs = [sci[2 * b] + sci[2 * b + 1] for b in range(NZ)]
     item_terms = []
@@ -590,17 +688,10 @@
         row = jnp.concatenate([pair[:, lanes] for pair in pairs], axis=1)
         item_terms.append(jnp.sum(mm(row_parts(row), gt[...], 1, 1), axis=0, keepdims=True))
     sdy[y, pl.ds(8, 8), :] = jnp.broadcast_to(item_terms[0], (8, 256))
-    sdx[t] = row_sums(dq_item.astype(F32) * q32[...]) + rs_row * item_terms[1]
+    rs_all = mm(jnp.ones((8, HD), BF16), lane_parts(rscol[...]), 1, 1)[0:1]
+    sdx[t] = dots + rs_all * item_terms[1]
     own_sdx = lambda peer: sdx.at[t]
     start3(x_copy, 5, own_sdx, sdx)
-    wait_in(x_from, 4, own_dqg, dqg)
-    gws_of = lambda peer: gws.at[peer]
-    acc = jnp.zeros((256, 1024), F32)
-    for tt in range(NT):
-        acc = acc + mm(dqg[tt], wt[2 * tt : 2 * tt + 2].reshape(256, 1024), 1, 0)
-    gws[...] = acc.astype(BF16).reshape(4, 64, 1024)
-    start3(y_copy, 2, gws_of, gwr)
-    gwr[y] = gws[y]
     wait_in(x_from, 5, own_sdx, sdx)
     sdy[y, pl.ds(0, 8), :] = sdx[0] + sdx[1] + sdx[2] + sdx[3]
     own_sdy = lambda peer: sdy.at[y]
@@ -616,7 +707,7 @@
     rs_own = rscol[mine, 0:1]
     wait_in(y_from, 4, own_sdy, sdy)
     last = sdy[0] + sdy[1] + sdy[2] + sdy[3]
-    sqm[...] = columns(2.0 * last[8:9] - (1.0 / D) * rs_row * rs_row * last[0:1])
+    sqm[...] = columns(2.0 * last[8:9] - (1.0 / D) * rs_all * rs_all * last[0:1])
     coef = sqm[mine, 0:1]
     direct = emb * coef
     wait_in(y_from, 2, gws_of, gwr)
@@ -630,13 +721,18 @@
         grad_ref[:, lanes] = er[q, :, halves[par]].astype(F32) + gw[:, lanes]
 
     for k, src, dst in (
-        (0, own_hd, hd), (1, own_sel, selb), (2, gws_of, gwr), (3, es_of, er), (4, own_sdy, sdy)
+        (0, own_hd, hd), (1, own_sel, selb), (2, gws_of, gwr), (3, es_of, er), (4, own_sdy, sdy),
+        (5, own_sqy, sqy),
     ):
         wait_out(y_copy, k, src, dst)
     for k, src, dst in (
-        (0, own_sqx, sqx), (4, own_dqg, dqg), (5, own_sdx, sdx)
+        (0, own_sqx, sqx), (5, own_sdx, sdx)
     ):
         wait_out(x_copy, k, src, dst)
+    for part in range(2):
+        for j in (1, 3, 2):
+            for copy in dq_copy(part, j):
+                copy.wait_send()
     for j in (1, 3, 2):
         ps_copy((t + j) % NT).wait_send()
     for u in range(4):
@@ -678,7 +774,8 @@
             vmem((4, 64, 1024), BF16),
             vmem((4, 1, 1024), F32),
             vmem((8, 2, 64, 1024), BF16),
-            vmem((4, 16, 256), F32),
+            vmem((4, 16, HIST), F32),
+            vmem((4, 8, HIST), F32),
             quarter(BF16),
             quarter(BF16),
             vmem((1024, 256), BF16),
@@ -706,6 +803,9 @@
             vmem((4, 512, 256), BF16),
             vmem((4, 512, 256), BF16),
             vmem((8, 512, HIST), BF16),
+            vmem((8, 512, HIST), BF16),
+            vmem((8, HIST, HIST), F32),
+            vmem((8, HIST, HIST), BF16),
             vmem((4, 512, 256), F32),
             vmem((4, 4, HIST, HIST), BF16),
             vmem((4, 2, HIST, HIST), F32),
@@ -725,23 +825,24 @@
             vmem((1024, 256), BF16),
             vmem((16, 1, 256), F32),
             vmem((16, 1, 256), F32),
-            quarter(BF16),
+            vmem((4, 4, 64, 256), BF16),
             vmem((4, 64, 1024), BF16),
             vmem((4, 64, 1024), BF16),
             vmem((4, 64, 256), BF16),
             vmem((4, 64, 256), BF16),
             vmem((4, 8, 256), F32),
             vmem((4, 16, 256), F32),
-            dma((10, 4)),
-            dma((10, 4)),
-            dma((5, 4)),
-            dma((5, 4)),
+            dma((11, 4)),
+            dma((11, 4)),
+            dma((6, 4)),
+            dma((6, 4)),
             dma((4, 4)),
             dma((4, 4)),
             dma((8, 2)),
             dma((8, 2)),
             dma((7,)),
             dma((7,)),
+            pltpu.SemaphoreType.REGULAR((2, 4)),
         ],
         compiler_params=pltpu.CompilerParams(
             collective_id=0, has_side_effects=True, vmem_limit_bytes=60 * 1024 * 1024

time: 119 us -> 103 us (0.87)
  Pallas kernels: 116 us -> 99.2 us
    pallas_call x1, Pallas kernels: 116 us -> 99.2 us  [local(): pl.pallas_call(kernel, out_shape=(jax.ShapeDtypeStruct((64, 1024), F32),...]
where the time goes in v4:
time: 103 us
  Pallas kernels  99.2 us (96%)
  local copies, waits for them, and re-layouts  2.95 us (3%)
    pallas_call x1, Pallas kernels, local(): pl.pallas_call(kernel, out_shape=(jax.ShapeDtypeStruct((64, 1024), F32),...  99.2 us
    unnamed x3, local copies, waits for them, and re-layouts  2.33 us

profile of v4, /device:TPU:1, one launch (start us, length us, event | category | flops | bytes accessed | tf_op | source)
XLA Modules:
  0.0 102.8 jit_solution(16321259455537784274)
XLA Ops:
  0.6 99.2 %shard_map.86 = (f32[64,1024]{1,0:T(8,128)}, f32[4,1,128]{2,1,0:T(1,128)}) custom-call(s32[4]{0:T(128)} %len_ref.1, bf16[64,1024]{1,0:T(8,128)(2,1)} %hidden_ref.1, bf16[64,1024]{1,0:T(8,128)(2,1)} %bitcast.4, bf16[1024]{0:T(1024)(128)(2,1)} %gi_ref.1, bf16[1024]{0:T(1024)(128)(2,1)} %gu_ref.1, s32[4,64]{1,0:T(4,128)} %bitcast.5, s32[4,192]{1,0:T(4,128)} %pos_ref.1), custom_call_target="tpu_custom_call" | custom-call | tf_op jit(solution)/shard_map/pallas_call | solution.py:761
  99.8 0.0 copy-start
  99.8 0.7 copy-done
  100.5 0.6 slice_reduce_fusion
  101.1 1.7 %copy.10 = f32[64,1024]{1,0:T(8,128)} copy(f32[64,1024]{1,0:T(8,128)} %get-tuple-element.8) | data formatting | bytes 524288
Async XLA Ops:
  99.8 0.7 copy-start

commit v5 on v4

--- a/solution.py
+++ b/solution.py
@@ -98,7 +98,7 @@
     rc_s, kn_s, v_s, qn_s, w_s, wt_s, p_t, ds_t, o_s, st_r, dsc, dneg_s, dnegt_s, gfol, grow,
     dout_t, dq_t, dk_s, dv_s, drc_s, nbs, dqo, eo, rq, re, sco, sci,
     dqg, gws, gwr, es, er, sdx, sdy,
-    xs, xr, ys, yr, ring_s, ring_r, par_s, par_r, a2a_s, a2a_r, hello,
+    xs, xr, ys, yr, ring_s, ring_r, par_s, par_r, a2a_s, a2a_r, ps_s, ps_r, hello,
 ):
     me = lax.axis_index("sect")
     t = lax.axis_index("tp")
@@ -160,7 +160,7 @@
             ).start()
             return carry
 
-        lax.fori_loop(1, NS, step, 0)
+        lax.fori_loop(1, NS, step, 0, unroll=7)
 
     def to_group(k, out, buf, group, same):
         def copy(j):
@@ -184,7 +184,7 @@
             copy(j).start()
             return carry
 
-        lax.fori_loop(1, 16, step, 0)
+        lax.fori_loop(1, 16, step, 0, unroll=5)
 
     def to_matched(k, src_of, dst):
         pltpu.make_async_copy(src_of(blk), dst.at[blk], a2a_r.at[k]).start()
@@ -196,7 +196,7 @@
             ).start()
             return carry
 
-        lax.fori_loop(1, 16, step, 0)
+        lax.fori_loop(1, 16, step, 0, unroll=5)
 
     def all_in(k, view):
         pltpu.make_async_copy(view, view, a2a_r.at[k]).wait()
@@ -330,21 +330,24 @@
     wait_in(y_from, 0, own_hd, hd)
     lhs = (hd[...].reshape(256, 1024).astype(F32) * (gi * gu)).astype(BF16)
 
-    near = z // 2
-    turn = 2 * (z % 2) - 1
-    order = (near, (near + turn + NT) % NT, (near - turn + NT) % NT, (near + 2) % NT)
-
-    def ps_copy(peer):
-        return send(ps.at[peer], pr.at[t], xs.at[1, peer], xr.at[1, t], me, peer)
-
-    def project(index):
-        part = order[index]
-        block = wt[pl.ds(2 * part, 2)].reshape(256, 1024)
-        ps[part] = mm(lhs, block, 1, 1).astype(BF16)
-
-        @pl.when(part != t)
+    def ps_copy(block):
+        part, par = block // 2, block % 2
+        return send(
+            ps.at[block], pr.at[t, par], ps_s.at[block], ps_r.at[t, par], me, part
+        )
+
+    def project(block):
+        ps[block] = mm(lhs, wt[block].reshape(HD, 1024), 1, 1).astype(BF16)
+
+        @pl.when(block // 2 != t)
         def _():
-            ps_copy(part).start()
+            ps_copy(block).start()
+
+    def project_step(step):
+        if step == 0:
+            project(z)
+        for way in (1, NZ - 1)[: 2 if step < 3 else 1]:
+            project((z + way * (step + 1)) % NZ)
 
     def partners_in(step):
         if step == 0:
@@ -356,7 +359,7 @@
                 partner_in((z + (NZ - way) * (step + 1)) % NZ, stream % 2)
 
     partners_in(0)
-    project(0)
+    project_step(0)
     wait_in(y_from, 1, own_sel, selb)
     picks = jnp.maximum(jnp.maximum(selb[0], selb[1]), jnp.maximum(selb[2], selb[3]))
     gt[...] = one_hot(picks.astype(jnp.int32), 256).astype(BF16)
@@ -382,29 +385,37 @@
         pieces.append((piece * rcol[...] * gain).astype(BF16))
     oute[...] = mm(gt[...], jnp.concatenate(pieces, axis=1), 0, 0).astype(BF16)
     partners_in(1)
-    project(1)
+    project_step(1)
     advance(2)
     relay(3)
     both = slice(0, 256)
     to_matched(5, lambda b: sqo.at[b // 2], sqi)
     to_readers(0, oute, bufe, both)
     partners_in(2)
-    project(2)
+    project_step(2)
     advance(3)
     partners_in(3)
-    project(3)
+    project_step(3)
     for q in range(4):
         gain_s[q] = jnp.concatenate(
             [gu[:, q * HD : (q + 1) * HD], gu[:, (4 + q) * HD : (5 + q) * HD]], axis=1
         )
-    pr[t] = ps[t]
-    for j in (1, 3, 2):
-        sender = (t + j) % NT
-        send(
-            ps.at[t], pr.at[sender], xs.at[1, sender], xr.at[1, sender], me, sender
-        ).wait_recv()
-    total = (
-        pr[0].astype(F32) + pr[1].astype(F32) + pr[2].astype(F32) + pr[3].astype(F32)
+    for par in range(2):
+        pr[t, par] = ps[2 * t + par]
+    for par in range(2):
+        for j in (1, 3, 2):
+            sender = (t + j) % NT
+            send(
+                ps.at[2 * t + par], pr.at[sender, par], ps_s.at[2 * t + par],
+                ps_r.at[sender, par], me, sender,
+            ).wait_recv()
+    total = jnp.concatenate(
+        [
+            pr[0, par].astype(F32) + pr[1, par].astype(F32)
+            + pr[2, par].astype(F32) + pr[3, par].astype(F32)
+            for par in range(2)
+        ],
+        axis=1,
     ) * (rcol[...] * rscol[...])[:, 0:1]
     q32[...] = total
     heads, _ = norm_heads(total)
@@ -634,6 +645,14 @@
 
     lax.fori_loop(0, 4, return_group, 0)
 
+    all_in(6, sci)
+    pairs = [sci[2 * b] + sci[2 * b + 1] for b in range(NZ)]
+    item_terms = []
+    for lanes in (slice(0, HD), slice(HD, 2 * HD)):
+        row = jnp.concatenate([pair[:, lanes] for pair in pairs], axis=1)
+        item_terms.append(jnp.sum(mm(row_parts(row), gt[...], 1, 1), axis=0, keepdims=True))
+    sdy[y, pl.ds(8, 8), :] = jnp.broadcast_to(item_terms[0], (8, 256))
+    rs_all = mm(jnp.ones((8, HD), BF16), lane_parts(rscol[...]), 1, 1)[0:1]
     all_in(2, rq)
     dq_item = norm_heads_back(q32[...], mm(gt[...], rq[...], 1, 0)).astype(BF16)
     dqg[t] = dq_item.reshape(4, 64, 256)
@@ -659,11 +678,13 @@
             for k, b in enumerate(chunks[part])
         ]
 
+    sdx[t] = row_sums(dq_item.astype(F32) * q32[...]) + rs_all * item_terms[1]
+    own_sdx = lambda peer: sdx.at[t]
+    start3(x_copy, 5, own_sdx, sdx)
     for part in range(2):
         for j in (2, 1, 3):
             for copy in dq_copy(part, j):
                 copy.start()
-    dots = row_sums(dq_item.astype(F32) * q32[...])
     gws_of = lambda peer: gws.at[peer]
     for part in range(2):
         for j in (1, 3, 2):
@@ -680,22 +701,12 @@
             gws[b] = acc[k * 64 : (k + 1) * 64]
         for j in ((2, 1), (3,))[part]:
             y_copy(2, gws_of, gwr, j).start()
+        if part == 0:
+            wait_in(x_from, 5, own_sdx, sdx)
+            sdy[y, pl.ds(0, 8), :] = sdx[0] + sdx[1] + sdx[2] + sdx[3]
+            own_sdy = lambda peer: sdy.at[y]
+            start3(y_copy, 4, own_sdy, sdy)
     gwr[y] = gws[y]
-    all_in(6, sci)
-    pairs = [sci[2 * b] + sci[2 * b + 1] for b in range(NZ)]
-    item_terms = []
-    for lanes in (slice(0, HD), slice(HD, 2 * HD)):
-        row = jnp.concatenate([pair[:, lanes] for pair in pairs], axis=1)
-        item_terms.append(jnp.sum(mm(row_parts(row), gt[...], 1, 1), axis=0, keepdims=True))
-    sdy[y, pl.ds(8, 8), :] = jnp.broadcast_to(item_terms[0], (8, 256))
-    rs_all = mm(jnp.ones((8, HD), BF16), lane_parts(rscol[...]), 1, 1)[0:1]
-    sdx[t] = dots + rs_all * item_terms[1]
-    own_sdx = lambda peer: sdx.at[t]
-    start3(x_copy, 5, own_sdx, sdx)
-    wait_in(x_from, 5, own_sdx, sdx)
-    sdy[y, pl.ds(0, 8), :] = sdx[0] + sdx[1] + sdx[2] + sdx[3]
-    own_sdy = lambda peer: sdy.at[y]
-    start3(y_copy, 4, own_sdy, sdy)
     all_in(3, re)
     es[...] = mm(gt[...], re[...], 1, 0).astype(BF16).reshape(4, 64, 256)
     es_of = lambda peer: es.at[peer]
@@ -734,7 +745,8 @@
             for copy in dq_copy(part, j):
                 copy.wait_send()
     for j in (1, 3, 2):
-        ps_copy((t + j) % NT).wait_send()
+        for par in range(2):
+            ps_copy((t + j) % NT * 2 + par).wait_send()
     for u in range(4):
         for j in (1, 3, 2):
             st_copy(u, j).wait_send()
@@ -776,8 +788,8 @@
             vmem((8, 2, 64, 1024), BF16),
             vmem((4, 16, HIST), F32),
             vmem((4, 8, HIST), F32),
-            quarter(BF16),
-            quarter(BF16),
+            vmem((8, 256, HD), BF16),
+            vmem((4, 2, 256, HD), BF16),
             vmem((1024, 256), BF16),
             vmem((1024, 256), BF16),
             quarter(BF16),
@@ -842,10 +854,12 @@
             dma((8, 2)),
             dma((7,)),
             dma((7,)),
+            dma((8,)),
+            dma((4, 2)),
             pltpu.SemaphoreType.REGULAR((2, 4)),
         ],
         compiler_params=pltpu.CompilerParams(
-            collective_id=0, has_side_effects=True, vmem_limit_bytes=60 * 1024 * 1024
+            collective_id=0, has_side_effects=True, vmem_limit_bytes=40 * 1024 * 1024
         ),
     )(
         hist_len, item_hidden, query_weight.T, item_gain, user_gain, send_item[0].T, pos_slot

time: 103 us -> 105 us (1.019)
  local copies, waits for them, and re-layouts: 2.95 us -> 5.85 us
    unnamed x3 -> x15, local copies, waits for them, and re-layouts: 2.33 us -> 5.23 us
where the time goes in v5:
time: 105 us
  Pallas kernels  98.4 us (94%)
  local copies, waits for them, and re-layouts  5.85 us (6%)
    pallas_call x1, Pallas kernels, local(): pl.pallas_call(kernel, out_shape=(jax.ShapeDtypeStruct((64, 1024), F32),...  98.4 us
    unnamed x15, local copies, waits for them, and re-layouts  5.23 us

profile of v5, /device:TPU:1, one launch (start us, length us, event | category | flops | bytes accessed | tf_op | source)
XLA Modules:
  0.0 104.9 jit_solution(15462214296021919386)
XLA Ops:
  0.6 0.0 copy-start.3
  0.6 0.0 copy-start.6
  0.7 0.7 copy-done.3
  1.3 0.0 copy-done.6
  1.3 0.0 copy-start
  1.3 0.9 copy-done
  2.2 0.0 copy-start.1
  2.2 0.9 copy-done.1
  3.1 0.0 copy-start.2
  3.1 0.7 copy-done.2
  3.8 0.0 copy-start.4
  3.8 0.7 copy-done.4
  4.5 0.0 copy-start.5
  4.5 0.7 copy-done.5
  5.2 98.4 %shard_map.86 = (f32[64,1024]{1,0:T(8,128)S(1)}, f32[4,1,128]{2,1,0:T(1,128)S(1)}) custom-call(s32[4]{0:T(128)S(1)} %copy-done.6, bf16[64,1024]{1,0:T(8,128)(2,1)S(1)} %copy-done, bf16[64,1024]{1,0:T(8,128)(2,1)S(1)} %bitcast.4, bf16[1024]{0:T(1024)(128)(2,1)S(1)} %copy-done.3, bf16[1024]{0:T(1024)(128)(2,1)S(1)} %copy-done.4, s32[4,64]{1,0:T(4,128)S(1)} %bitcast.5, ...), custom_call_target="tpu_custom_call" | custom-call | tf_op jit(solution)/shard_map/pallas_call | solution.py:773
  103.6 0.6 slice_reduce_fusion
  104.2 0.7 copy.10
Async XLA Ops:
  0.6 0.7 copy-start.3
  0.6 0.7 copy-start.6
  1.3 0.9 copy-start
  2.2 0.9 copy-start.1
  3.1 0.7 copy-start.2
  3.8 0.7 copy-start.4
  4.5 0.7 copy-start.5

commit v6 on v5

--- a/solution.py
+++ b/solution.py
@@ -91,8 +91,9 @@
 
 
 def kernel(
-    len_ref, hidden_ref, w_ref, gi_ref, gu_ref, send_ref, pos_ref,
+    len_in, hidden_in, w_in, gi_in, gu_in, send_in, pos_in,
     grad_ref, loss_ref,
+    len_ref, hidden_ref, gi_ref, gu_ref, send_ref, pos_ref, in_sem,
     hd, selb, wt, sqx, sqy, ps, pr, oute, outq, bufe, bufq, gt, nrm, knb, sqo, sqi, sqm, rsm, q32,
     rcol, rscol, pos_s, hot, hott, sqf_s, sqc_s, gain_s,
     rc_s, kn_s, v_s, qn_s, w_s, wt_s, p_t, ds_t, o_s, st_r, dsc, dneg_s, dnegt_s, gfol, grow,
@@ -253,9 +254,21 @@
     for j in range(1, NT):
         pl.semaphore_signal(barrier, inc=1, device_id=(me, (t + j) % NT), device_id_type=MESH)
 
-    hd[y] = hidden_ref[...]
+    loads = [
+        pltpu.make_async_copy(src, dst, in_sem.at[k])
+        for k, (src, dst) in enumerate(
+            (
+                (send_in, send_ref), (w_in, wt.at[z, c]), (hidden_in, hd.at[y]),
+                (gi_in, gi_ref), (gu_in, gu_ref), (hidden_in, hidden_ref), (pos_in, pos_ref),
+                (len_in, len_ref),
+            )
+        )
+    ]
+    for load in loads:
+        load.start()
+    for load in loads:
+        load.wait()
     sqx[t] = jnp.zeros((16, HIST), F32)
-    wt[z, c] = w_ref[...]
     spread = jnp.where((iota((64, 1024), 1) >> 4) == iota((64, 1024), 0), 1.0, 0.0).astype(BF16)
     named = mm(send_ref[...].astype(F32).astype(BF16), spread, 1, 0)
     lane = iota((1, 1024), 1)
@@ -643,7 +656,6 @@
         to_group(3, eo, re, (y + 1 + i) % 4, i == 3)
         return carry
 
-    lax.fori_loop(0, 4, return_group, 0)
 
     all_in(6, sci)
     pairs = [sci[2 * b] + sci[2 * b + 1] for b in range(NZ)]
@@ -654,6 +666,7 @@
     sdy[y, pl.ds(8, 8), :] = jnp.broadcast_to(item_terms[0], (8, 256))
     rs_all = mm(jnp.ones((8, HD), BF16), lane_parts(rscol[...]), 1, 1)[0:1]
     all_in(2, rq)
+    lax.fori_loop(0, 4, return_group, 0)
     dq_item = norm_heads_back(q32[...], mm(gt[...], rq[...], 1, 0)).astype(BF16)
     dqg[t] = dq_item.reshape(4, 64, 256)
     chunks = (((y + 2) % NY, (y + 1) % NY), ((y + 3) % NY, y))
@@ -699,13 +712,13 @@
         acc = acc.astype(BF16)
         for k, b in enumerate(chunks[part]):
             gws[b] = acc[k * 64 : (k + 1) * 64]
-        for j in ((2, 1), (3,))[part]:
-            y_copy(2, gws_of, gwr, j).start()
         if part == 0:
             wait_in(x_from, 5, own_sdx, sdx)
             sdy[y, pl.ds(0, 8), :] = sdx[0] + sdx[1] + sdx[2] + sdx[3]
             own_sdy = lambda peer: sdy.at[y]
             start3(y_copy, 4, own_sdy, sdy)
+        for j in ((2, 1), (3,))[part]:
+            y_copy(2, gws_of, gwr, j).start()
     gwr[y] = gws[y]
     all_in(3, re)
     es[...] = mm(gt[...], re[...], 1, 0).astype(BF16).reshape(4, 64, 256)
@@ -776,13 +789,19 @@
             jax.ShapeDtypeStruct((64, 1024), F32),
             jax.ShapeDtypeStruct((4, 1, HIST), F32),
         ),
-        in_specs=[pl.BlockSpec(memory_space=pltpu.SMEM)]
-        + [pl.BlockSpec(memory_space=pltpu.VMEM)] * 6,
+        in_specs=[pl.BlockSpec(memory_space=pltpu.HBM)] * 7,
         out_specs=(
             pl.BlockSpec(memory_space=pltpu.VMEM),
             pl.BlockSpec(memory_space=pltpu.VMEM),
         ),
         scratch_shapes=[
+            pltpu.SMEM((4,), jnp.int32),
+            vmem((64, 1024), BF16),
+            vmem((1024,), BF16),
+            vmem((1024,), BF16),
+            vmem((4, 64), jnp.int32),
+            vmem((4, HIST + CAND), jnp.int32),
+            dma((8,)),
             vmem((4, 64, 1024), BF16),
             vmem((4, 1, 1024), F32),
             vmem((8, 2, 64, 1024), BF16),
@@ -862,7 +881,13 @@
             collective_id=0, has_side_effects=True, vmem_limit_bytes=40 * 1024 * 1024
         ),
     )(
-        hist_len, item_hidden, query_weight.T, item_gain, user_gain, send_item[0].T, pos_slot
+        *[
+            pltpu.with_memory_space_constraint(value, pltpu.HBM)
+            for value in (
+                hist_len, item_hidden, query_weight.T, item_gain, user_gain, send_item[0].T,
+                pos_slot,
+            )
+        ]
     )
     return (grad, loss[:, 0, 0])
 

time: 105 us -> 99.5 us (0.948)
  local copies, waits for them, and re-layouts: 5.85 us -> 1.33 us
    unnamed x15 -> x1, local copies, waits for them, and re-layouts: 5.23 us -> 0.7 us
where the time goes in v6:
time: 99.5 us; the launch traced here: 99.4 us
  Pallas kernels  97.4 us (98%)
  local copies, waits for them, and re-layouts  1.33 us (1%)
    pallas_call x1, Pallas kernels, local(): pl.pallas_call(kernel, out_shape=(jax.ShapeDtypeStruct((64, 1024), F32),...  97.4 us

profile of v6, /device:TPU:1, one launch (start us, length us, event | category | flops | bytes accessed | tf_op | source)
XLA Modules:
  0.0 99.4 jit_solution(4802151247449647966)
XLA Ops:
  0.6 97.4 %shard_map.86 = (f32[64,1024]{1,0:T(8,128)S(1)}, f32[4,1,128]{2,1,0:T(1,128)S(1)}) custom-call(s32[4]{0:T(128)} %len_in.1, bf16[64,1024]{1,0:T(8,128)(2,1)} %hidden_in.1, bf16[64,1024]{1,0:T(8,128)(2,1)} %bitcast.4, bf16[1024]{0:T(1024)(128)(2,1)} %gi_in.1, bf16[1024]{0:T(1024)(128)(2,1)} %gu_in.1, s32[4,64]{1,0:T(4,128)} %bitcast.5, s32[4,192]{1,0:T(4,128)} %pos_in.1), custom_call_target="tpu_custom_call" | custom-call | tf_op jit(solution)/shard_map/pallas_call | solution.py:786
  98.0 0.6 slice_reduce_fusion
  98.6 0.7 copy.10

commit v7 on v6

--- a/solution.py
+++ b/solution.py
@@ -79,6 +79,12 @@
     return heads, roots
 
 
+def head_back(values, grad):
+    root = lax.rsqrt(lane_sum(values * values) * (1.0 / HD) + EPS)
+    head = values * root
+    return root * (grad - head * (lane_sum(grad * head) * (1.0 / HD)))
+
+
 def norm_heads_back(values, grads):
     heads, roots = norm_heads(values)
     out = []
@@ -98,7 +104,7 @@
     rcol, rscol, pos_s, hot, hott, sqf_s, sqc_s, gain_s,
     rc_s, kn_s, v_s, qn_s, w_s, wt_s, p_t, ds_t, o_s, st_r, dsc, dneg_s, dnegt_s, gfol, grow,
     dout_t, dq_t, dk_s, dv_s, drc_s, nbs, dqo, eo, rq, re, sco, sci,
-    dqg, gws, gwr, es, er, sdx, sdy,
+    dqg, acc_s, gws, gwr, es, er, sdx, sdy,
     xs, xr, ys, yr, ring_s, ring_r, par_s, par_r, a2a_s, a2a_r, ps_s, ps_r, hello,
 ):
     me = lax.axis_index("sect")
@@ -163,18 +169,18 @@
 
         lax.fori_loop(1, NS, step, 0, unroll=7)
 
-    def to_group(k, out, buf, group, same):
+    def to_group(k, out, buf, group, same, lanes):
         def copy(j):
             b = (blk + j) % 16
             return send(
-                out.at[group, rows_of(b)], buf.at[rows_of(me)],
+                out.at[group, rows_of(b), lanes], buf.at[rows_of(me), lanes],
                 a2a_s.at[k], a2a_r.at[k], sect_of(b // 2, group, b % 2), t,
             )
 
         @pl.when(same)
         def _():
             pltpu.make_async_copy(
-                out.at[group, rows_of(blk)], buf.at[rows_of(me)], a2a_r.at[k]
+                out.at[group, rows_of(blk), lanes], buf.at[rows_of(me), lanes], a2a_r.at[k]
             ).start()
 
         @pl.when(jnp.logical_not(same))
@@ -587,44 +593,48 @@
 
     lax.fori_loop(0, 4, losses, 0)
 
-    def backward_quarter(i, carry):
+    def backward_step(par, i):
         q = (y + 1 + i) % 4
-        for u in range(4):
-            span = slice(u * HIST, (u + 1) * HIST)
+        lanes = halves[par]
+        spans = [(slice(u * HIST, (u + 1) * HIST), u) for u in range(4)]
+        for span, u in spans:
             cspan = slice((4 + u) * HIST, (5 + u) * HIST)
-            dhit = twice(dsc[u, 1])
-            out = o_s[q, span]
-            rows = rc_s[q, span].astype(F32)
+            dhit = dsc[u, 1]
+            out = o_s[q, span, lanes]
+            rows = rc_s[q, span, lanes].astype(F32)
             dout = (
-                twice(dsc[u, 0]) * out
+                dsc[u, 0] * out
                 + dhit * follow_of(rows)
-                + mm(dneg_s[u], rc_s[q, cspan], 1, 0)
+                + mm(dneg_s[u], rc_s[q, cspan, lanes], 1, 0)
             )
-            dout_t[span] = dout.astype(BF16)
-            drc_s[q, span] = (dout + pltpu.roll(dhit * out, 1, 0)).astype(BF16)
-            drc_s[q, cspan] = mm(dnegt_s[u], out.astype(BF16), 1, 0).astype(BF16)
-        tasks = [
-            (slice(u * HIST, (u + 1) * HIST), halves[par], par, 2 * u + par)
-            for u in range(4)
-            for par in range(2)
-        ]
-        for span, lanes, par, slot in tasks:
-            p_t[slot] = mm(dout_t[span, lanes], v_s[q, span, lanes], 1, 1)
-        for span, lanes, par, slot in tasks:
-            dw = p_t[slot]
+            dout_t[span, lanes] = dout.astype(BF16)
+            drc_s[q, span, lanes] = (dout + pltpu.roll(dhit * out, 1, 0)).astype(BF16)
+            drc_s[q, cspan, lanes] = mm(dnegt_s[u], out.astype(BF16), 1, 0).astype(BF16)
+        for span, u in spans:
+            p_t[u] = mm(dout_t[span, lanes], v_s[q, span, lanes], 1, 1)
+        for span, u in spans:
+            dw = p_t[u]
             wide = w_s[2 * q + par, span].astype(F32)
-            ds_t[slot] = (wide * (dw - lane_sum(dw * wide)) * scale).astype(BF16)
-        for span, lanes, par, slot in tasks:
-            dq_t[span, lanes] = mm(ds_t[slot], kn_s[q, span, lanes], 1, 0).astype(BF16)
-            dk_s[q, span, lanes] = mm(ds_t[slot], qn_s[q, span, lanes], 0, 0).astype(BF16)
+            ds_t[u] = (wide * (dw - lane_sum(dw * wide)) * scale).astype(BF16)
+        for span, u in spans:
+            dq_t[span, lanes] = mm(ds_t[u], kn_s[q, span, lanes], 1, 0).astype(BF16)
+            dk_s[q, span, lanes] = mm(ds_t[u], qn_s[q, span, lanes], 0, 0).astype(BF16)
             dv_s[q, span, lanes] = mm(wt_s[2 * q + par, span], dout_t[span, lanes], 1, 0).astype(
                 BF16
             )
-        dqo[q] = mm(hot[:, 0:512], dq_t[...], 1, 0).astype(BF16)
-        to_group(2, dqo, rq, q, i == 3)
+        dqo[q, :, lanes] = mm(hot[:, 0:512], dq_t[:, lanes], 1, 0).astype(BF16)
+        to_group((2, 7)[par], dqo, rq, q, i == 3, lanes)
+
+    def backward_first(i, carry):
+        backward_step(0, i)
         return carry
 
-    lax.fori_loop(0, 4, backward_quarter, 0)
+    def backward_second(i, carry):
+        backward_step(1, i)
+        return carry
+
+    lax.fori_loop(0, 4, backward_first, 0)
+    lax.fori_loop(0, 4, backward_second, 0)
 
     nbs[...] = jnp.zeros(nbs.shape, F32)
 
@@ -653,10 +663,35 @@
     to_matched(6, lambda b: sco.at[b], sci)
 
     def return_group(i, carry):
-        to_group(3, eo, re, (y + 1 + i) % 4, i == 3)
+        to_group(3, eo, re, (y + 1 + i) % 4, i == 3, both)
         return carry
 
 
+    chunks = (((y + 2) % NY, (y + 1) % NY), ((y + 3) % NY, y))
+
+    def dq_first(peer, sender):
+        return send(
+            dqg.at[t, 0], dqg.at[sender, 0], xs.at[2, peer], xr.at[2, sender], me, peer
+        )
+
+    def dq_second(part, k, peer, sender):
+        b = chunks[part][k]
+        index = (1, 3, 4, 10)[2 * part + k]
+        return send(
+            dqg.at[t, 1, b], dqg.at[sender, 1, b], xs.at[index, peer], xr.at[index, sender],
+            me, peer,
+        )
+
+    def item_dq(par):
+        lanes = halves[par]
+        out = head_back(q32[:, lanes], mm(gt[...], rq[:, lanes], 1, 0)).astype(BF16)
+        dqg[t, par] = out.reshape(4, 64, HD)
+        return row_sums(out.astype(F32) * q32[:, lanes])
+
+    all_in(2, rq.at[:, halves[0]])
+    dots = item_dq(0)
+    for j in (2, 1, 3):
+        dq_first((t + j) % NT, t).start()
     all_in(6, sci)
     pairs = [sci[2 * b] + sci[2 * b + 1] for b in range(NZ)]
     item_terms = []
@@ -665,49 +700,34 @@
         item_terms.append(jnp.sum(mm(row_parts(row), gt[...], 1, 1), axis=0, keepdims=True))
     sdy[y, pl.ds(8, 8), :] = jnp.broadcast_to(item_terms[0], (8, 256))
     rs_all = mm(jnp.ones((8, HD), BF16), lane_parts(rscol[...]), 1, 1)[0:1]
-    all_in(2, rq)
-    lax.fori_loop(0, 4, return_group, 0)
-    dq_item = norm_heads_back(q32[...], mm(gt[...], rq[...], 1, 0)).astype(BF16)
-    dqg[t] = dq_item.reshape(4, 64, 256)
-    chunks = (((y + 2) % NY, (y + 1) % NY), ((y + 3) % NY, y))
-
-    def dq_copy(part, j):
-        peer = (t + j) % NT
-        return [
-            send(
-                dqg.at[t, b], dqg.at[t, b], xs.at[(2, 3, 4, 10)[2 * part + k], peer],
-                xr.at[(2, 3, 4, 10)[2 * part + k], t], me, peer,
-            )
-            for k, b in enumerate(chunks[part])
-        ]
-
-    def dq_from(part, j):
-        sender = (t + NT - j) % NT
-        return [
-            send(
-                dqg.at[t, b], dqg.at[sender, b], xs.at[(2, 3, 4, 10)[2 * part + k], sender],
-                xr.at[(2, 3, 4, 10)[2 * part + k], sender], me, sender,
-            )
-            for k, b in enumerate(chunks[part])
-        ]
-
-    sdx[t] = row_sums(dq_item.astype(F32) * q32[...]) + rs_all * item_terms[1]
+    all_in(7, rq.at[:, halves[1]])
+    dots = dots + item_dq(1)
+    sdx[t] = dots + rs_all * item_terms[1]
     own_sdx = lambda peer: sdx.at[t]
     start3(x_copy, 5, own_sdx, sdx)
     for part in range(2):
         for j in (2, 1, 3):
-            for copy in dq_copy(part, j):
-                copy.start()
+            for k in range(2):
+                dq_second(part, k, (t + j) % NT, t).start()
+    lax.fori_loop(0, 4, return_group, 0)
+    for j in (1, 3, 2):
+        sender = (t + j) % NT
+        dq_first(sender, sender).wait_recv()
+    acc = jnp.zeros((256, 1024), F32)
+    for tt in range(NT):
+        acc = acc + mm(dqg[tt, 0].reshape(256, HD), wt[2 * tt].reshape(HD, 1024), 1, 0)
+    acc_s[...] = acc.reshape(4, 64, 1024)
     gws_of = lambda peer: gws.at[peer]
     for part in range(2):
         for j in (1, 3, 2):
-            for copy in dq_from(part, j):
-                copy.wait_recv()
-        acc = jnp.zeros((128, 1024), F32)
+            sender = (t + j) % NT
+            for k in range(2):
+                dq_second(part, k, sender, sender).wait_recv()
+        acc = jnp.concatenate([acc_s[b] for b in chunks[part]], axis=0)
         for tt in range(NT):
             acc = acc + mm(
-                jnp.concatenate([dqg[tt, b] for b in chunks[part]], axis=0),
-                wt[2 * tt : 2 * tt + 2].reshape(256, 1024), 1, 0,
+                jnp.concatenate([dqg[tt, 1, b] for b in chunks[part]], axis=0),
+                wt[2 * tt + 1].reshape(HD, 1024), 1, 0,
             )
         acc = acc.astype(BF16)
         for k, b in enumerate(chunks[part]):
@@ -753,10 +773,12 @@
         (0, own_sqx, sqx), (5, own_sdx, sdx)
     ):
         wait_out(x_copy, k, src, dst)
-    for part in range(2):
-        for j in (1, 3, 2):
-            for copy in dq_copy(part, j):
-                copy.wait_send()
+    for j in (1, 3, 2):
+        peer = (t + j) % NT
+        dq_first(peer, t).wait_send()
+        for part in range(2):
+            for k in range(2):
+                dq_second(part, k, peer, t).wait_send()
     for j in (1, 3, 2):
         for par in range(2):
             ps_copy((t + j) % NT * 2 + par).wait_send()
@@ -773,7 +795,8 @@
     all_out(0, oute.at[most])
     all_out(1, outq.at[most, halves[0]])
     all_out(4, outq.at[most, halves[1]])
-    all_out(2, rq.at[most])
+    all_out(2, rq.at[most, halves[0]])
+    all_out(7, rq.at[most, halves[1]])
     all_out(3, re.at[most])
     all_out(5, sqi.at[pl.ds(0, 15)])
     all_out(6, sci.at[pl.ds(0, 15)])
@@ -856,7 +879,8 @@
             vmem((1024, 256), BF16),
             vmem((16, 1, 256), F32),
             vmem((16, 1, 256), F32),
-            vmem((4, 4, 64, 256), BF16),
+            vmem((4, 2, 4, 64, HD), BF16),
+            vmem((4, 64, 1024), F32),
             vmem((4, 64, 1024), BF16),
             vmem((4, 64, 1024), BF16),
             vmem((4, 64, 256), BF16),
@@ -871,8 +895,8 @@
             dma((4, 4)),
             dma((8, 2)),
             dma((8, 2)),
-            dma((7,)),
-            dma((7,)),
+            dma((8,)),
+            dma((8,)),
             dma((8,)),
             dma((4, 2)),
             pltpu.SemaphoreType.REGULAR((2, 4)),

time: 99.5 us -> 101 us (1.015)
  Pallas kernels: 97.4 us -> 98.9 us
    pallas_call x1, Pallas kernels: 97.4 us -> 98.9 us  [local(): pl.pallas_call(kernel, out_shape=(jax.ShapeDtypeStruct((64, 1024), F32),...]
where the time goes in v7:
time: 101 us
  Pallas kernels  98.9 us (98%)
  local copies, waits for them, and re-layouts  1.33 us (1%)
    pallas_call x1, Pallas kernels, local(): pl.pallas_call(kernel, out_shape=(jax.ShapeDtypeStruct((64, 1024), F32),...  98.9 us

profile of v7, /device:TPU:1, one launch (start us, length us, event | category | flops | bytes accessed | tf_op | source)
XLA Modules:
  0.0 100.9 jit_solution(15575315058404919174)
XLA Ops:
  0.6 98.9 %shard_map.86 = (f32[64,1024]{1,0:T(8,128)S(1)}, f32[4,1,128]{2,1,0:T(1,128)S(1)}) custom-call(s32[4]{0:T(128)} %len_in.1, bf16[64,1024]{1,0:T(8,128)(2,1)} %hidden_in.1, bf16[64,1024]{1,0:T(8,128)(2,1)} %bitcast.4, bf16[1024]{0:T(1024)(128)(2,1)} %gi_in.1, bf16[1024]{0:T(1024)(128)(2,1)} %gu_in.1, s32[4,64]{1,0:T(4,128)} %bitcast.5, s32[4,192]{1,0:T(4,128)} %pos_in.1), custom_call_target="tpu_custom_call" | custom-call | tf_op jit(solution)/shard_map/pallas_call | solution.py:809
  99.6 0.6 slice_reduce_fusion
  100.2 0.7 copy.10

commit v8 on v7

--- a/solution.py
+++ b/solution.py
@@ -594,10 +594,13 @@
     lax.fori_loop(0, 4, losses, 0)
 
     def backward_step(par, i):
-        q = (y + 1 + i) % 4
         lanes = halves[par]
-        spans = [(slice(u * HIST, (u + 1) * HIST), u) for u in range(4)]
-        for span, u in spans:
+        tasks = [
+            ((y + 1 + 2 * i + k) % 4, k, slice(u * HIST, (u + 1) * HIST), u, 4 * k + u)
+            for k in range(2)
+            for u in range(4)
+        ]
+        for q, k, span, u, slot in tasks:
             cspan = slice((4 + u) * HIST, (5 + u) * HIST)
             dhit = dsc[u, 1]
             out = o_s[q, span, lanes]
@@ -607,23 +610,24 @@
                 + dhit * follow_of(rows)
                 + mm(dneg_s[u], rc_s[q, cspan, lanes], 1, 0)
             )
-            dout_t[span, lanes] = dout.astype(BF16)
+            dout_t[k, span] = dout.astype(BF16)
             drc_s[q, span, lanes] = (dout + pltpu.roll(dhit * out, 1, 0)).astype(BF16)
             drc_s[q, cspan, lanes] = mm(dnegt_s[u], out.astype(BF16), 1, 0).astype(BF16)
-        for span, u in spans:
-            p_t[u] = mm(dout_t[span, lanes], v_s[q, span, lanes], 1, 1)
-        for span, u in spans:
-            dw = p_t[u]
+        for q, k, span, u, slot in tasks:
+            p_t[slot] = mm(dout_t[k, span], v_s[q, span, lanes], 1, 1)
+        for q, k, span, u, slot in tasks:
+            dw = p_t[slot]
             wide = w_s[2 * q + par, span].astype(F32)
-            ds_t[u] = (wide * (dw - lane_sum(dw * wide)) * scale).astype(BF16)
-        for span, u in spans:
-            dq_t[span, lanes] = mm(ds_t[u], kn_s[q, span, lanes], 1, 0).astype(BF16)
-            dk_s[q, span, lanes] = mm(ds_t[u], qn_s[q, span, lanes], 0, 0).astype(BF16)
-            dv_s[q, span, lanes] = mm(wt_s[2 * q + par, span], dout_t[span, lanes], 1, 0).astype(
-                BF16
-            )
-        dqo[q, :, lanes] = mm(hot[:, 0:512], dq_t[:, lanes], 1, 0).astype(BF16)
-        to_group((2, 7)[par], dqo, rq, q, i == 3, lanes)
+            ds_t[slot] = (wide * (dw - lane_sum(dw * wide)) * scale).astype(BF16)
+        for q, k, span, u, slot in tasks:
+            dq_t[k, span] = mm(ds_t[slot], kn_s[q, span, lanes], 1, 0).astype(BF16)
+            dk_s[q, span, lanes] = mm(ds_t[slot], qn_s[q, span, lanes], 0, 0).astype(BF16)
+            dv_s[q, span, lanes] = mm(wt_s[2 * q + par, span], dout_t[k, span], 1, 0).astype(BF16)
+        for k in range(2):
+            q = tasks[4 * k][0]
+            dqo[q, :, lanes] = mm(hot[:, 0:512], dq_t[k], 1, 0).astype(BF16)
+        for k in range(2):
+            to_group((2, 7)[par], dqo, rq, tasks[4 * k][0], i + k == 2, lanes)
 
     def backward_first(i, carry):
         backward_step(0, i)
@@ -633,8 +637,8 @@
         backward_step(1, i)
         return carry
 
-    lax.fori_loop(0, 4, backward_first, 0)
-    lax.fori_loop(0, 4, backward_second, 0)
+    lax.fori_loop(0, 2, backward_first, 0)
+    lax.fori_loop(0, 2, backward_second, 0)
 
     nbs[...] = jnp.zeros(nbs.shape, F32)
 
@@ -688,6 +692,7 @@
         dqg[t, par] = out.reshape(4, 64, HD)
         return row_sums(out.astype(F32) * q32[:, lanes])
 
+    lax.fori_loop(0, 4, return_group, 0)
     all_in(2, rq.at[:, halves[0]])
     dots = item_dq(0)
     for j in (2, 1, 3):
@@ -709,7 +714,6 @@
         for j in (2, 1, 3):
             for k in range(2):
                 dq_second(part, k, (t + j) % NT, t).start()
-    lax.fori_loop(0, 4, return_group, 0)
     for j in (1, 3, 2):
         sender = (t + j) % NT
         dq_first(sender, sender).wait_recv()
@@ -867,8 +871,8 @@
             vmem((4, HIST, HIST), BF16),
             vmem((512, HIST), F32),
             vmem((4, 1, HIST), F32),
-            vmem((512, 256), BF16),
-            vmem((512, 256), BF16),
+            vmem((2, 512, HD), BF16),
+            vmem((2, 512, HD), BF16),
             vmem((4, 512, 256), BF16),
             vmem((4, 512, 256), BF16),
             vmem((4, 1024, 256), BF16),

time: 101 us -> 98.1 us (0.971)
  Pallas kernels: 98.9 us -> 96 us
    pallas_call x1, Pallas kernels: 98.9 us -> 96 us  [local(): pl.pallas_call(kernel, out_shape=(jax.ShapeDtypeStruct((64, 1024), F32),...]
where the time goes in v8:
time: 98.1 us; the launch traced here: 98 us
  Pallas kernels  96 us (98%)
  local copies, waits for them, and re-layouts  1.33 us (1%)
    pallas_call x1, Pallas kernels, local(): pl.pallas_call(kernel, out_shape=(jax.ShapeDtypeStruct((64, 1024), F32),...  96 us

profile of v8, /device:TPU:1, one launch (start us, length us, event | category | flops | bytes accessed | tf_op | source)
XLA Modules:
  0.0 98.0 jit_solution(8361799583006311000)
XLA Ops:
  0.6 96.0 %shard_map.86 = (f32[64,1024]{1,0:T(8,128)S(1)}, f32[4,1,128]{2,1,0:T(1,128)S(1)}) custom-call(s32[4]{0:T(128)} %len_in.1, bf16[64,1024]{1,0:T(8,128)(2,1)} %hidden_in.1, bf16[64,1024]{1,0:T(8,128)(2,1)} %bitcast.4, bf16[1024]{0:T(1024)(128)(2,1)} %gi_in.1, bf16[1024]{0:T(1024)(128)(2,1)} %gu_in.1, s32[4,64]{1,0:T(4,128)} %bitcast.5, s32[4,192]{1,0:T(4,128)} %pos_in.1), custom_call_target="tpu_custom_call" | custom-call | tf_op jit(solution)/shard_map/pallas_call | solution.py:813
  96.6 0.6 slice_reduce_fusion
  97.3 0.7 copy.10

commit v9 on v8

--- a/solution.py
+++ b/solution.py
@@ -538,18 +538,23 @@
         score(2 * i + 1)
         return carry
 
-    def turn_weights(k, carry):
-        for u in range(4):
-            span = slice(u * HIST, (u + 1) * HIST)
-            wt_s[k, span] = jnp.transpose(w_s[k, span].astype(F32)).astype(BF16)
-        return carry
+    def turn_weights(par):
+        def step(q, carry):
+            for u in range(4):
+                span = slice(u * HIST, (u + 1) * HIST)
+                wt_s[2 * q + par, span] = jnp.transpose(
+                    w_s[2 * q + par, span].astype(F32)
+                ).astype(BF16)
+            return carry
+
+        lax.fori_loop(0, 4, step, 0)
 
     for par, step in ((0, first_half), (1, second_half)):
         all_in(1 if par == 0 else 4, outq.at[:, halves[0]])
         for q in range(4):
             qn_s[q, :, halves[par]] = mm(hott[0:512], bufq[q, :, halves[par]], 1, 0).astype(BF16)
         lax.fori_loop(0, 2, step, 0)
-    lax.fori_loop(0, 8, turn_weights, 0)
+        turn_weights(par)
 
     def losses(u, carry):
         for j in (1, 3, 2):
@@ -697,6 +702,12 @@
     dots = item_dq(0)
     for j in (2, 1, 3):
         dq_first((t + j) % NT, t).start()
+    all_in(7, rq.at[:, halves[1]])
+    dots = dots + item_dq(1)
+    for part in range(2):
+        for j in (2, 1, 3):
+            for k in range(2):
+                dq_second(part, k, (t + j) % NT, t).start()
     all_in(6, sci)
     pairs = [sci[2 * b] + sci[2 * b + 1] for b in range(NZ)]
     item_terms = []
@@ -705,15 +716,9 @@
         item_terms.append(jnp.sum(mm(row_parts(row), gt[...], 1, 1), axis=0, keepdims=True))
     sdy[y, pl.ds(8, 8), :] = jnp.broadcast_to(item_terms[0], (8, 256))
     rs_all = mm(jnp.ones((8, HD), BF16), lane_parts(rscol[...]), 1, 1)[0:1]
-    all_in(7, rq.at[:, halves[1]])
-    dots = dots + item_dq(1)
     sdx[t] = dots + rs_all * item_terms[1]
     own_sdx = lambda peer: sdx.at[t]
     start3(x_copy, 5, own_sdx, sdx)
-    for part in range(2):
-        for j in (2, 1, 3):
-            for k in range(2):
-                dq_second(part, k, (t + j) % NT, t).start()
     for j in (1, 3, 2):
         sender = (t + j) % NT
         dq_first(sender, sender).wait_recv()

time: 98.1 us -> 97.5 us (level)
  no operation moved by 1% of the time
where the time goes in v9:
time: 97.5 us; the launch traced here: 97.4 us
  Pallas kernels  95.4 us (98%)
  local copies, waits for them, and re-layouts  1.33 us (1%)
    pallas_call x1, Pallas kernels, local(): pl.pallas_call(kernel, out_shape=(jax.ShapeDtypeStruct((64, 1024), F32),...  95.4 us

profile of v9, /device:TPU:1, one launch (start us, length us, event | category | flops | bytes accessed | tf_op | source)
XLA Modules:
  0.0 97.4 jit_solution(5507428926493302257)
XLA Ops:
  0.6 95.4 %shard_map.86 = (f32[64,1024]{1,0:T(8,128)S(1)}, f32[4,1,128]{2,1,0:T(1,128)S(1)}) custom-call(s32[4]{0:T(128)} %len_in.1, bf16[64,1024]{1,0:T(8,128)(2,1)} %hidden_in.1, bf16[64,1024]{1,0:T(8,128)(2,1)} %bitcast.4, bf16[1024]{0:T(1024)(128)(2,1)} %gi_in.1, bf16[1024]{0:T(1024)(128)(2,1)} %gu_in.1, s32[4,64]{1,0:T(4,128)} %bitcast.5, s32[4,192]{1,0:T(4,128)} %pos_in.1), custom_call_target="tpu_custom_call" | custom-call | tf_op jit(solution)/shard_map/pallas_call | solution.py:818
  96.1 0.6 slice_reduce_fusion
  96.7 0.7 copy.10

commit v10 on v9

--- a/solution.py
+++ b/solution.py
@@ -556,9 +556,7 @@
         lax.fori_loop(0, 2, step, 0)
         turn_weights(par)
 
-    def losses(u, carry):
-        for j in (1, 3, 2):
-            st_from(u, j).wait_recv()
+    def losses(u):
         stats = (
             st_r[0, u].astype(F32) + st_r[1, u].astype(F32)
             + st_r[2, u].astype(F32) + st_r[3, u].astype(F32)
@@ -594,9 +592,16 @@
         dsqf = jnp.broadcast_to(-0.5 * dtl * tl * rf * rf, (HIST, HIST))
         gfol[user_rows(u)] = pltpu.roll(dsqf, 1, 0)
         grow[u] = -0.5 * rc * rc * jnp.sum(dnl * nl, axis=0, keepdims=True)
+
+    def losses_pair(i, carry):
+        for k in range(2):
+            for j in (1, 3, 2):
+                st_from(2 * i + k, j).wait_recv()
+        for k in range(2):
+            losses(2 * i + k)
         return carry
 
-    lax.fori_loop(0, 4, losses, 0)
+    lax.fori_loop(0, 2, losses_pair, 0)
 
     def backward_step(par, i):
         lanes = halves[par]

time: 97.5 us -> 98 us (level)
  no operation moved by 1% of the time
where the time goes in v10:
time: 98 us; the launch traced here: 97.9 us
  Pallas kernels  96 us (98%)
  local copies, waits for them, and re-layouts  1.33 us (1%)
    pallas_call x1, Pallas kernels, local(): pl.pallas_call(kernel, out_shape=(jax.ShapeDtypeStruct((64, 1024), F32),...  96 us

profile of v10, /device:TPU:1, one launch (start us, length us, event | category | flops | bytes accessed | tf_op | source)
XLA Modules:
  0.0 97.9 jit_solution(8836688703712521425)
XLA Ops:
  0.6 96.0 %shard_map.86 = (f32[64,1024]{1,0:T(8,128)S(1)}, f32[4,1,128]{2,1,0:T(1,128)S(1)}) custom-call(s32[4]{0:T(128)} %len_in.1, bf16[64,1024]{1,0:T(8,128)(2,1)} %hidden_in.1, bf16[64,1024]{1,0:T(8,128)(2,1)} %bitcast.4, bf16[1024]{0:T(1024)(128)(2,1)} %gi_in.1, bf16[1024]{0:T(1024)(128)(2,1)} %gu_in.1, s32[4,64]{1,0:T(4,128)} %bitcast.5, s32[4,192]{1,0:T(4,128)} %pos_in.1), custom_call_target="tpu_custom_call" | custom-call | tf_op jit(solution)/shard_map/pallas_call | solution.py:823
  96.6 0.6 slice_reduce_fusion
  97.2 0.7 copy.10
